TPU v7x, 128 devices: a whole 4x4x4 slice. The times are simulated.
128 devices in a mesh: leaf: 8 (over y_lo, z), front: 16 (over x, y_hi, core).
Axes of the slice: x: 4, y: 4 (y_hi: 2, y_lo: 2; y = y_hi * 2 + y_lo), z: 4, core: 2. Of those that a mesh axis runs over, the one named last changes fastest.
Arguments:
- leaf_fronts: float32 [32768, 4096], P('leaf', 'front'), as said below
- root_front: float32 [4096, 16, 256], P(None, 'front', 'leaf'), as said below
- leaf_order: int32 [8, 16], P('leaf'), may hold values from 0 to 15, each once within a row
- leaf_map: int32 [8, 16], P('leaf'), may hold values from 0 to 15, each once within a row
- root_order: int32 [16], replicated, may hold values from 0 to 15, each once
Outputs:
- leaf_factor: float32 [32768, 4096], P('leaf', 'front')
- root_factor: float32 [4096, 16, 256], P(None, 'front', 'leaf')
Inputs may be any that keep to these rules, and one draw needn't show every extreme that they name: `leaf_fronts`: each leaf block of 4096 rows is symmetric and positive definite. `root_front`: symmetric and positive definite. `leaf_order`: each row names every block column once. `leaf_map`: each row names every root block once. `root_order`: names every block column once.
All inputs are finite; a program needn't handle non-finite values.
Results may differ from a plain program's by a relative error of at most 0.00018.
Values sent between devices are 32-bit elements; how exact they have to be, the bound alone decides.
A program may use at most 128 MiB of HBM per device.

v0:
```python
import jax
import jax.numpy as jnp
from jax import lax
from jax.sharding import PartitionSpec as P

NPIV = 2


def spread(value, axis, root):
    mine = lax.axis_index(axis) == root
    return lax.psum(jnp.where(mine, value, jnp.zeros_like(value)), axis)


def invert(permutation):
    block_ids = jnp.arange(permutation.shape[0], dtype=jnp.int32)
    hits = permutation[None, :] == block_ids[:, None]
    return jnp.sum(jnp.where(hits, block_ids[None, :], 0), axis=1)


def make_panel(raw_column, pivot_block, alive_set, block_size):
    block_count = raw_column.shape[0] // block_size
    tile_stack = raw_column.reshape(block_count, block_size, block_size)
    diag_block = lax.dynamic_index_in_dim(tile_stack, pivot_block, 0, keepdims=False)
    lower_factor = jnp.linalg.cholesky(diag_block)
    solved = lax.linalg.triangular_solve(
        lower_factor, raw_column, left_side=False, lower=True, transpose_a=True
    )
    keep_rows = alive_set & (jnp.arange(block_count, dtype=jnp.int32) != pivot_block)
    solved = jnp.where(jnp.repeat(keep_rows, block_size)[:, None], solved, 0.0)
    tile_stack = solved.reshape(block_count, block_size, block_size)
    tile_stack = lax.dynamic_update_index_in_dim(tile_stack, lower_factor, pivot_block, 0)
    return tile_stack.reshape(block_count * block_size, block_size)


def owner_panel(raw_column, pivot_block, alive_set, my_block, block_size):
    return lax.cond(
        my_block == pivot_block,
        lambda whole: make_panel(whole, pivot_block, alive_set, block_size),
        lambda whole: jnp.zeros_like(whole),
        raw_column,
    )


def spread_root(panel_here, pivot_block):
    return spread(panel_here, "front", pivot_block)


def advance(
    column, factor_panel, pivot_block, alive_set, my_block, row_start, column_start, own_width
):
    own_rows = lax.dynamic_slice_in_dim(factor_panel, row_start, own_width, 0)
    updated = column - jnp.dot(factor_panel, own_rows.T, precision=lax.Precision.HIGHEST)
    own_panel = lax.dynamic_slice_in_dim(factor_panel, column_start, own_width, 1)
    mine_alive = alive_set[my_block]
    column = jnp.where(my_block == pivot_block, own_panel, jnp.where(mine_alive, updated, column))
    block_ids = jnp.arange(alive_set.shape[0], dtype=jnp.int32)
    return (column, alive_set & (block_ids != pivot_block))


def shards(leaf_fronts, root_front, leaf_order, leaf_map, root_order):
    block_size = leaf_fronts.shape[1]
    order_rows = leaf_fronts.shape[0]
    block_count = lax.axis_size("front")
    my_block = lax.axis_index("front")
    leaf_index = lax.axis_index("leaf")
    slice_width = root_front.shape[2]
    column = leaf_fronts
    alive_set = jnp.ones((block_count,), dtype=jnp.bool_)
    for position in range(NPIV):
        pivot_block = leaf_order[0, position]
        panel_here = owner_panel(column, pivot_block, alive_set, my_block, block_size)
        factor_panel = spread(panel_here, "front", pivot_block)
        column, alive_set = advance(
            column,
            factor_panel,
            pivot_block,
            alive_set,
            my_block,
            my_block * block_size,
            0,
            block_size,
        )
    mine_alive = alive_set[my_block]
    row_alive = jnp.repeat(alive_set, block_size)
    leaf_out = jnp.where(mine_alive & ~row_alive[:, None], 0.0, column)
    contribution = jnp.where(mine_alive, leaf_out, 0.0)
    flipped = jnp.swapaxes(contribution.reshape(block_count, block_size, block_size), 1, 2)
    inverse = invert(leaf_map[0])
    outgoing = jnp.take(flipped, inverse, axis=0)
    incoming = lax.all_to_all(outgoing, "front", split_axis=0, concat_axis=0, tiled=True)
    gathered_tiles = jnp.take(incoming, inverse, axis=0).reshape(order_rows, block_size)
    root_slice = root_front[:, 0, :]
    root_alive = jnp.ones((block_count,), dtype=jnp.bool_)
    root_part = (
        lax.psum_scatter(gathered_tiles, "leaf", scatter_dimension=1, tiled=True) + root_slice
    )
    position = 0
    pivot_block = root_order[position]
    raw_column = lax.all_gather(root_part, "leaf", axis=1, tiled=True)
    panel_here = owner_panel(raw_column, pivot_block, root_alive, my_block, block_size)
    factor_panel = spread_root(panel_here, pivot_block)
    root_part, root_alive = advance(
        root_part,
        factor_panel,
        pivot_block,
        root_alive,
        my_block,
        my_block * block_size + leaf_index * slice_width,
        leaf_index * slice_width,
        slice_width,
    )
    mine_root = root_alive[my_block]
    root_rows = jnp.repeat(root_alive, block_size)
    root_part = jnp.where(mine_root & ~root_rows[:, None], 0.0, root_part)
    return (leaf_out, root_part[:, None, :])


def solution(mesh):
    return jax.shard_map(
        shards,
        mesh=mesh,
        in_specs=(
            P("leaf", "front"),
            P(None, "front", "leaf"),
            P("leaf", None),
            P("leaf", None),
            P(),
        ),
        out_specs=(P("leaf", "front"), P(None, "front", "leaf")),
        check_vma=False,
    )
```

profile of v0, /device:TPU:1, one launch (start us, length us, event | category | flops | bytes accessed | tf_op | source)
XLA Modules:
  0.0 967.2 jit_solution(2211953817270246410)
XLA Ops:
  7.2 0.0 all-reduce.5.cloned.1.call-start
  7.2 1.3 fusion.45
  9.2 6.0 conditional.3
  9.2 2.3 broadcast.102
  15.2 2.3 broadcast_select_fusion.5
  17.5 0.0 all-reduce.5.cloned.1.call-update
  17.5 0.0 all-reduce.7.cloned.1.call-start
  18.2 0.7 iota_compare_fusion.13
  18.9 234.1 %all-reduce.5.cloned.1.call-done = f32[4096,256]{1,0:T(8,128)} async-done(((f32[4096,256]{1,0:T(8,128)}), f32[4096,256]{1,0:T(8,128)}) %all-reduce.5.cloned.1.call-update) | async-done | bytes 4194320 | tf_op jit(solution)/shard_map/psum | solution.py:11
  252.9 10.2 %fusion.31 = f32[4096,256]{1,0:T(8,128)} fusion(f32[4096,256]{1,0:T(8,128)} %all-reduce.5.cloned.1.call-done, f32[4096,256]{1,0:T(8,128)} %param.16, pred[]{:T(512)S(6)} %eq.15, s32[]{:T(128)S(6)} %select_n.119), kind=kOutput, calls=%fused_computation.101 | convolution fusion | flops 3223322624 | bytes 17039364 | tf_op jit(solution)/shard_map/dot_general | solution.py:52
  263.2 7.6 conditional.4
  263.2 2.2 broadcast.108
  270.8 2.3 broadcast_select_fusion.4
  273.0 0.0 all-reduce.7.cloned.1.call-update
  273.1 0.0 reduce-scatter.4.cloned.1.call-start
  273.1 0.6 dynamic_slice.33
  273.7 1.3 compare_and_fusion.2
  275.0 0.6 dynamic_slice.31
  275.5 1.8 not_and_fusion.1
  277.4 0.1 broadcast_in_dim.112
  277.5 0.1 select_reduce_fusion.6
  277.6 223.5 %all-reduce.7.cloned.1.call-done = f32[4096,256]{1,0:T(8,128)} async-done(((f32[4096,256]{1,0:T(8,128)}), f32[4096,256]{1,0:T(8,128)}) %all-reduce.7.cloned.1.call-update) | async-done | bytes 4194320 | tf_op jit(solution)/shard_map/psum | solution.py:11
  501.1 10.6 %broadcast_select_fusion.3 = (f32[4096,256]{1,0:T(8,128)}, f32[4096,256]{1,0:T(8,128)}) fusion(pred[]{:T(512)} %bitcast.35, f32[4096,256]{1,0:T(8,128)} %all-reduce.7.cloned.1.call-done, f32[4096,256]{1,0:T(8,128)} %fusion.31, s32[]{:T(128)S(6)} %select_n.119, pred[]{:T(512)} %bitcast.36, pred[]{:T(512)S(6)} %eq.14, pred[4096]{0:T(1024)(128)(4,1)S(1)} %and.45), kind=kOutput, calls=%fused_computation.111 | convolution fusion | flops 3226468352 | bytes 21238788 | tf_op jit(solution)/shard_map/dot_general | solution.py:52
  511.7 4.9 gather_fusion
  516.7 2.8 broadcast_select_fusion.1
  519.5 57.9 %all_to_all.5 = f32[16,256,256]{1,2,0:T(8,128)} all-to-all(f32[16,256,256]{1,2,0:T(8,128)S(1)} %broadcast_select_fusion.1), channel_id=1, replica_groups=mesh['leaf'=8,'front'=16] {'front'}, dimensions={0} | all-to-all | bytes 8388608 | tf_op jit(solution)/shard_map/all_to_all | solution.py:90
  577.4 5.0 gather_fusion.1
  582.4 4.6 broadcast_select_fusion
  587.0 5.3 copy.44
  592.3 5.6 copy.54
  598.0 0.0 all-gather.2.cloned.1.call-start
  598.0 1.0 copy-done.4
  599.0 1.9 copy.45
  600.9 48.6 %reduce-scatter.4.cloned.1.call-done = f32[32,4096]{1,0:T(8,128)} async-done(((f32[256,4096]{1,0:T(8,128)}), f32[32,4096]{1,0:T(8,128)}) %reduce-scatter.4.cloned.1.call-update) | async-done | bytes 524304
  649.6 3.0 copy.55
  652.6 2.4 bitcast_add_fusion.3
  655.0 1.4 copy.46
  656.4 0.0 all-reduce.9.cloned.1.call-start
  656.5 51.5 %all-gather.2.cloned.1.call-done = f32[4096,256]{0,1:T(8,128)} async-done(((f32[4096,32]{0,1:T(8,128)}), f32[4096,256]{0,1:T(8,128)}) %all-gather.2.cloned.1.call-update) | async-done | bytes 4194320 | tf_op jit(solution)/shard_map/all_gather | solution.py:99
  708.0 4.9 conditional.5
  708.0 2.2 broadcast.112
  712.9 2.3 broadcast_select_fusion.2
  715.3 0.6 dynamic_slice.35
  715.9 0.7 not_and_fusion
  716.5 0.1 broadcast_in_dim.115
  716.6 234.4 %all-reduce.9.cloned.1.call-done = f32[4096,256]{1,0:T(8,128)} async-done(((f32[4096,256]{1,0:T(8,128)}), f32[4096,256]{1,0:T(8,128)}) %all-reduce.9.cloned.1.call-update) | async-done | bytes 4194320 | tf_op jit(solution)/shard_map/psum | solution.py:11
  951.0 6.5 fusion.35
  957.5 3.0 copy.49
  (14 shorter events, 0.1 us)
Async XLA Ops:
  7.2 245.8 %all-reduce.5.cloned.1.call-start = ((), (), s32[]{:S(2)}) async-start(), calls=%async_computation.2 | async-start | bytes 8388608 | tf_op jit(solution)/shard_map/psum | solution.py:11
  17.5 483.6 %all-reduce.7.cloned.1.call-start = ((), (), s32[]{:S(2)}) async-start(), calls=%async_computation.3 | async-start | bytes 8388608 | tf_op jit(solution)/shard_map/psum | solution.py:11
  273.0 4.4 copy-start.6
  273.1 376.5 %reduce-scatter.4.cloned.1.call-start = ((), (), s32[]{:S(2)}) async-start(), calls=%async_computation.6 | async-start | bytes 4718592
  598.0 1.0 copy-start.4
  598.0 110.0 %all-gather.2.cloned.1.call-start = ((), (), s32[]{:S(2)}) async-start(), calls=%async_computation.4 | async-start | bytes 4718592 | tf_op jit(solution)/shard_map/all_gather | solution.py:99
  652.6 3.9 copy-start.5
  656.4 294.6 %all-reduce.9.cloned.1.call-start = ((), (), s32[]{:S(2)}) async-start(), calls=%async_computation.5 | async-start | bytes 8388608 | tf_op jit(solution)/shard_map/psum | solution.py:11
Sparse Core Ops, SparseCore 0:
  17.7 235.2 all-reduce.4
  273.2 227.9 all-reduce.6
  598.1 51.4 reduce-scatter.3
  656.5 51.4 all-gather.1
  715.3 235.6 all-reduce.8
where the time goes:
time: 977 us; the launch traced here: 967 us
  waiting for transfers between devices  792 us (81%)
  blocking collectives  57.9 us (6%)
  local copies, waits for them, and re-layouts  41.2 us (4%)
  matrix products  27.3 us (3%)
  other arithmetic  21.3 us (2%)
  between operations  15.4 us (2%)
  loops' own time  11.8 us (1%)
    psum x3, waiting for transfers between devices, spread(): return lax.psum(jnp.where(mine, value, jnp.zeros_like(value)), axis)  692 us
    all_to_all x1, blocking collectives, shards(): lax.all_to_all(outgoing, 'front', split_axis=0, concat_axis=0, tiled=True)  57.9 us
    all_gather x1, waiting for transfers between devices, shards(): raw_column = lax.all_gather(root_part, 'leaf', axis=1, tiled=True)  51.5 us
    unnamed x6, waiting for transfers between devices  48.7 us
    dot_general x3, matrix products, advance(): jnp.dot(factor_panel, own_rows.T, precision=lax.Precision.HIGHEST)  27.3 us
  transfers between devices with their start and end apart: 5, of which 5 were waited for; matrix products, arithmetic and copies ran while one was open for 1% of the time, Pallas kernels for 0%

commit v1 on v0

v1 whole, which is shorter than its diff:
```python
import jax
import jax.numpy as jnp
from jax import lax
from jax.sharding import PartitionSpec as P

HIGH = lax.Precision.HIGH


def invert(permutation):
    block_ids = jnp.arange(permutation.shape[0], dtype=jnp.int32)
    hits = permutation[None, :] == block_ids[:, None]
    return jnp.sum(jnp.where(hits, block_ids[None, :], 0), axis=1)


def make_panel(raw_column, pivot_block, alive_set):
    block_size = raw_column.shape[1]
    block_count = raw_column.shape[0] // block_size
    diag_block = lax.dynamic_slice_in_dim(raw_column, pivot_block * block_size, block_size, 0)
    lower = jnp.linalg.cholesky(diag_block)
    solved = lax.linalg.triangular_solve(
        lower, raw_column, left_side=False, lower=True, transpose_a=True
    )
    block_ids = jnp.arange(block_count, dtype=jnp.int32)
    keep = (alive_set & (block_ids != pivot_block))[:, None, None]
    tiles = solved.reshape(block_count, block_size, block_size)
    on_pivot = (block_ids == pivot_block)[:, None, None]
    tiles = jnp.where(on_pivot, lower[None], jnp.where(keep, tiles, 0.0))
    return tiles.reshape(block_count * block_size, block_size)


def block_row(tiles, pivot_block):
    return lax.dynamic_index_in_dim(tiles, pivot_block, 0, keepdims=False)


def shards(leaf_fronts, root_front, leaf_order, leaf_map, root_order):
    order_rows, block_size = leaf_fronts.shape
    block_count = order_rows // block_size
    my_block = lax.axis_index("front")
    leaf_index = lax.axis_index("leaf")
    slice_width = root_front.shape[2]
    block_ids = jnp.arange(block_count, dtype=jnp.int32)
    own_start = my_block * block_size

    tiles = leaf_fronts.reshape(block_count, block_size, block_size)
    first, second = leaf_order[0, 0], leaf_order[0, 1]
    raw_first = lax.all_gather(block_row(tiles, first).T, "front", axis=0, tiled=True)
    raw_second = lax.all_gather(block_row(tiles, second).T, "front", axis=0, tiled=True)
    everything = jnp.ones((block_count,), dtype=jnp.bool_)
    panel_first = make_panel(raw_first, first, everything)
    alive = block_ids != first
    pivot_rows = lax.dynamic_slice_in_dim(panel_first, second * block_size, block_size, 0)
    raw_second = raw_second - jnp.dot(panel_first, pivot_rows.T, precision=HIGH)
    panel_second = make_panel(raw_second, second, alive)
    alive = alive & (block_ids != second)

    own_first = lax.dynamic_slice_in_dim(panel_first, own_start, block_size, 0)
    own_second = lax.dynamic_slice_in_dim(panel_second, own_start, block_size, 0)
    updated = (
        leaf_fronts
        - jnp.dot(panel_first, own_first.T, precision=HIGH)
        - jnp.dot(panel_second, own_second.T, precision=HIGH)
    )
    updated = updated.reshape(block_count, block_size, block_size)
    updated = jnp.where(alive[:, None, None], updated, 0.0)
    leaf_out = jnp.where(
        my_block == first,
        panel_first,
        jnp.where(my_block == second, panel_second, updated.reshape(order_rows, block_size)),
    )

    mine_alive = alive[my_block]
    inverse = invert(leaf_map[0])
    outgoing = jnp.take(jnp.where(mine_alive, updated, 0.0), inverse, axis=0)
    incoming = lax.all_to_all(outgoing, "front", split_axis=0, concat_axis=0, tiled=True)
    gathered = jnp.swapaxes(jnp.take(incoming, inverse, axis=0), 0, 1)
    gathered = gathered.reshape(block_size, order_rows)
    part = lax.psum_scatter(gathered, "leaf", scatter_dimension=0, tiled=True)
    part = part + root_front[:, 0, :].T

    pivot = root_order[0]
    row = lax.dynamic_slice_in_dim(part, pivot * block_size, block_size, 1)
    raw_root = lax.all_gather(row, ("front", "leaf"), axis=0, tiled=True)
    panel = make_panel(raw_root, pivot, everything)
    own = lax.dynamic_slice_in_dim(panel, own_start + leaf_index * slice_width, slice_width, 0)
    part = part - jnp.dot(own, panel.T, precision=HIGH)
    part = part.reshape(slice_width, block_count, block_size)
    part = jnp.where((block_ids != pivot)[None, :, None], part, 0.0)
    part = part.reshape(slice_width, order_rows)
    own_panel = lax.dynamic_slice_in_dim(panel, leaf_index * slice_width, slice_width, 1)
    root_out = jnp.where(my_block == pivot, own_panel, part.T)
    return (leaf_out, root_out[:, None, :])


def solution(mesh):
    return jax.shard_map(
        shards,
        mesh=mesh,
        in_specs=(
            P("leaf", "front"),
            P(None, "front", "leaf"),
            P("leaf", None),
            P("leaf", None),
            P(),
        ),
        out_specs=(P("leaf", "front"), P(None, "front", "leaf")),
        check_vma=False,
    )
```

time: 977 us -> 792 us (0.81)
  waiting for transfers between devices: 792 us -> 403 us
  other arithmetic: 21.3 us -> 187 us
  local copies, waits for them, and re-layouts: 41.2 us -> 72.4 us
  matrix products: 27.3 us -> 40.5 us
  loops' own time: 11.8 us -> 0.15 us
    psum x3 -> x0, waiting for transfers between devices: 692 us -> none  [spread(): return lax.psum(jnp.where(mine, value, jnp.zeros_like(value)), axis)]
    all_gather x1 -> x3, waiting for transfers between devices: 51.5 us -> 351 us  [the longest x1 300 us: shards(): raw_root = lax.all_gather(row, ('front', 'leaf'), axis=0, tiled=True)]
    another operation x0 -> x27, other arithmetic: none -> 163 us  [the longest x20 103 us: make_panel(): lower = jnp.linalg.cholesky(diag_block)]
    reduce_scatter x0 -> x1, waiting for transfers between devices: none -> 51.2 us  [shards(): part = lax.psum_scatter(gathered, 'leaf', scatter_dimension=0, tiled=True)]
    unnamed x6 -> x4, waiting for transfers between devices: 48.7 us -> 0.74 us
    another operation x0 -> x15, matrix products: none -> 24.2 us  [the longest x9 22.8 us: make_panel(): lax.linalg.triangular_solve(lower, raw_column, left_side=False, lower=Tru...]
    unnamed x10 -> x25, local copies, waits for them, and re-layouts: 14.5 us -> 31.1 us
    another operation x3, loops' own time: 11.8 us -> 0.15 us  [make_panel(): lax.linalg.triangular_solve(lower, raw_column, left_side=False, lower=Tru...]
  transfers between devices with their start and end apart: 5 -> 4, of which waited for: 5 -> 3; matrix products, arithmetic and copies ran while one was open for 1% -> 11% of each run, Pallas kernels for 0% -> 0%
where the time goes in v1:
time: 792 us; the launch traced here: 781 us
  waiting for transfers between devices  403 us (51%)
  other arithmetic  187 us (24%)
  local copies, waits for them, and re-layouts  72.4 us (9%)
  blocking collectives  54.1 us (7%)
  matrix products  40.5 us (5%)
  between operations  24.1 us (3%)
    all_gather x1, waiting for transfers between devices, shards(): raw_root = lax.all_gather(row, ('front', 'leaf'), axis=0, tiled=True)  300 us
    another operation x20, other arithmetic, make_panel(): lower = jnp.linalg.cholesky(diag_block)  103 us
    another operation x7, other arithmetic, make_panel(): lax.linalg.triangular_solve(lower, raw_column, left_side=False, lower=Tru...  60.1 us
    all_to_all x1, blocking collectives, shards(): lax.all_to_all(outgoing, 'front', split_axis=0, concat_axis=0, tiled=True)  54.1 us
    all_gather x1, waiting for transfers between devices, shards(): lax.all_gather(block_row(tiles, first).T, 'front', axis=0, tiled=True)  51.5 us
    reduce_scatter x1, waiting for transfers between devices, shards(): part = lax.psum_scatter(gathered, 'leaf', scatter_dimension=0, tiled=True)  51.2 us
    unnamed x25, local copies, waits for them, and re-layouts  31.1 us
    another operation x9, matrix products, make_panel(): lax.linalg.triangular_solve(lower, raw_column, left_side=False, lower=Tru...  22.8 us
  transfers between devices with their start and end apart: 4, of which 3 were waited for; matrix products, arithmetic and copies ran while one was open for 11% of the time, Pallas kernels for 0%

profile of v1, /device:TPU:1, one launch (start us, length us, event | category | flops | bytes accessed | tf_op | source)
XLA Modules:
  0.0 781.4 jit_solution(6167048104012507612)
XLA Ops:
  11.8 1.9 dynamic-slice_bitcast_fusion
  16.7 5.6 copy.75
  25.0 51.5 %all-gather.4.cloned.1.call-done = f32[4096,256]{0,1:T(8,128)} async-done(((f32[256,256]{0,1:T(8,128)}), f32[4096,256]{0,1:T(8,128)}) %all-gather.4.cloned.1.call-update) | async-done | bytes 4194320 | tf_op jit(solution)/shard_map/all_gather | solution.py:46
  78.7 11.7 %cholesky.172 = f32[128,128]{1,0:T(8,128)S(1)} custom-call(f32[128,128]{1,0:T(8,128)S(1)} %cholesky.270), custom_call_target="Cholesky" | custom-call | tf_op jit(solution)/shard_map/jit(cholesky)/cholesky | solution.py:19
  90.4 9.8 %custom-call.15 = f32[1,128,128]{1,2,0:T(8,128)S(1)} custom-call(f32[1,128,128]{2,1,0:T(8,128)S(1)} %get-tuple-element.87), custom_call_target="InvertDiagBlocksLowerTriangular" | custom-call | tf_op jit(solution)/shard_map/jit(cholesky)/cholesky | solution.py:19
  100.7 11.7 %cholesky.189 = f32[128,128]{1,0:T(8,128)S(1)} custom-call(f32[128,128]{1,0:T(8,128)S(1)} %convolution_subtract_fusion.9), custom_call_target="Cholesky" | custom-call | tf_op jit(solution)/shard_map/jit(cholesky)/cholesky | solution.py:19
  114.6 3.8 while.6
  118.4 20.0 %custom-call.16 = f32[2,128,128]{1,2,0:T(8,128)S(1)} custom-call(f32[2,128,128]{2,1,0:T(8,128)S(1)} %get-tuple-element.25), custom_call_target="InvertDiagBlocksLowerTriangular" | custom-call | tf_op jit(solution)/shard_map/triangular_solve/custom-call.0 | solution.py:20
  138.8 3.9 copy.94
  142.6 1.9 fusion.11
  144.6 2.1 convolution_subtract_fusion.5
  146.6 2.0 fusion.31
  148.6 2.8 fusion.4
  151.5 5.7 convolution_subtract_fusion.2
  157.2 2.0 copy-done.1
  160.3 11.7 %cholesky.206 = f32[128,128]{1,0:T(8,128)S(1)} custom-call(f32[128,128]{1,0:T(8,128)S(1)} %cholesky.273), custom_call_target="Cholesky" | custom-call | tf_op jit(solution)/shard_map/jit(cholesky)/cholesky | solution.py:19
  172.7 9.8 %custom-call.17 = f32[1,128,128]{1,2,0:T(8,128)S(1)} custom-call(f32[1,128,128]{2,1,0:T(8,128)S(1)} %get-tuple-element.83), custom_call_target="InvertDiagBlocksLowerTriangular" | custom-call | tf_op jit(solution)/shard_map/jit(cholesky)/cholesky | solution.py:19
  183.0 11.7 %cholesky.223 = f32[128,128]{1,0:T(8,128)S(1)} custom-call(f32[128,128]{1,0:T(8,128)S(1)} %convolution_subtract_fusion.8), custom_call_target="Cholesky" | custom-call | tf_op jit(solution)/shard_map/jit(cholesky)/cholesky | solution.py:19
  197.0 4.1 while.7
  201.1 20.1 %custom-call.18 = f32[2,128,128]{1,2,0:T(8,128)S(1)} custom-call(f32[2,128,128]{2,1,0:T(8,128)S(1)} %get-tuple-element.26), custom_call_target="InvertDiagBlocksLowerTriangular" | custom-call | tf_op jit(solution)/shard_map/triangular_solve/custom-call.0 | solution.py:20
  221.2 3.6 fusion.9
  224.8 2.0 convolution_subtract_fusion.4
  226.8 2.0 fusion.27
  229.2 3.9 copy.95
  233.1 2.2 convolution_subtract_fusion.1
  236.1 6.2 select_select_fusion.1
  242.3 5.6 copy.90
  247.9 5.3 select_select_fusion
  253.2 4.9 gather_fusion
  258.1 2.8 broadcast_select_fusion
  260.9 54.1 %all_to_all.5 = f32[16,256,256]{2,1,0:T(8,128)} all-to-all(f32[16,256,256]{2,1,0:T(8,128)S(1)} %broadcast_select_fusion), channel_id=1, replica_groups=mesh['leaf'=8,'front'=16] {'front'}, dimensions={0} | all-to-all | bytes 8388608 | tf_op jit(solution)/shard_map/all_to_all | solution.py:74
  315.1 5.0 gather_fusion.1
  320.1 4.7 select_bitcast_fusion
  324.8 5.3 copy.79
  330.1 5.6 copy.91
  336.4 51.2 %reduce-scatter.4.cloned.1.call-done = f32[32,4096]{1,0:T(8,128)} async-done(((f32[256,4096]{1,0:T(8,128)}), f32[32,4096]{1,0:T(8,128)}) %reduce-scatter.4.cloned.1.call-update) | async-done | bytes 524304 | tf_op jit(solution)/shard_map/reduce_scatter | solution.py:77
  389.6 5.6 copy.84
  395.2 300.0 %all-gather.8.cloned.1.call-done = f32[4096,256]{1,0:T(8,128)} async-done(((f32[32,256]{1,0:T(8,128)}), f32[4096,256]{1,0:T(8,128)}) %all-gather.8.cloned.1.call-update) | async-done | bytes 4194320 | tf_op jit(solution)/shard_map/all_gather | solution.py:82
  697.4 11.7 %cholesky.240 = f32[128,128]{1,0:T(8,128)S(1)} custom-call(f32[128,128]{1,0:T(8,128)S(1)} %cholesky.276), custom_call_target="Cholesky" | custom-call | tf_op jit(solution)/shard_map/jit(cholesky)/cholesky | solution.py:19
  709.7 9.8 %custom-call.19 = f32[1,128,128]{1,2,0:T(8,128)S(1)} custom-call(f32[1,128,128]{2,1,0:T(8,128)S(1)} %get-tuple-element.79), custom_call_target="InvertDiagBlocksLowerTriangular" | custom-call | tf_op jit(solution)/shard_map/jit(cholesky)/cholesky | solution.py:19
  720.1 11.7 %cholesky.257 = f32[128,128]{1,0:T(8,128)S(1)} custom-call(f32[128,128]{1,0:T(8,128)S(1)} %convolution_subtract_fusion.7), custom_call_target="Cholesky" | custom-call | tf_op jit(solution)/shard_map/jit(cholesky)/cholesky | solution.py:19
  734.1 4.1 while.8
  738.1 19.9 %custom-call.20 = f32[2,128,128]{1,2,0:T(8,128)S(1)} custom-call(f32[2,128,128]{2,1,0:T(8,128)S(1)} %get-tuple-element.27), custom_call_target="InvertDiagBlocksLowerTriangular" | custom-call | tf_op jit(solution)/shard_map/triangular_solve/custom-call.0 | solution.py:20
  758.0 3.7 fusion.7
  761.7 3.5 convolution_subtract_fusion.3
  765.3 2.0 fusion.23
  767.6 3.8 copy.96
  772.2 2.2 fusion.3
  (115 shorter events, 32.8 us)
Async XLA Ops:
  7.2 69.4 %all-gather.4.cloned.1.call-start = ((), (), s32[]{:S(2)}) async-start(), calls=%async_computation.2 | async-start | bytes 4456448 | tf_op jit(solution)/shard_map/all_gather | solution.py:46
  13.6 137.8 %all-gather.6.cloned.1.call-start = ((), (), s32[]{:S(2)}) async-start(), calls=%async_computation.3 | async-start | bytes 4456448 | tf_op jit(solution)/shard_map/all_gather | solution.py:47
  14.4 373.2 %reduce-scatter.4.cloned.1.call-start = ((), (), s32[]{:S(2)}) async-start(), calls=%async_computation.5 | async-start | bytes 4718592 | tf_op jit(solution)/shard_map/reduce_scatter | solution.py:77
  16.6 8.2 %copy-start.7 = (s32[1,16]{1,0:T(1,128)S(1)}, s32[1,16]{1,0:T(1,128)}, u32[]{:S(2)}) copy-start(s32[1,16]{1,0:T(1,128)} %param.13) | copy-start | bytes 196
  138.8 3.9 copy-start.4
  157.2 2.0 copy-start.1
  221.1 3.7 copy-start.2
  229.2 3.9 copy-start
  229.2 3.9 copy-start.3
  335.7 0.7 copy-start.8
  335.7 51.9 %copy-start.6 = (f32[4096,1,32]{0,2,1:T(8,128)S(1)}, f32[4096,1,32]{0,2,1:T(8,128)}, u32[]{:S(2)}) copy-start(f32[4096,1,32]{0,2,1:T(8,128)} %param.11) | copy-start | bytes 1572868
  335.7 359.5 %all-gather.8.cloned.1.call-start = ((), (), s32[]{:S(2)}) async-start(), calls=%async_computation.4 | async-start | bytes 4227072 | tf_op jit(solution)/shard_map/all_gather | solution.py:82
  758.0 3.7 copy-start.5
Sparse Core Ops, SparseCore 0:
  13.8 62.7 all-gather.3
  79.4 58.3 all-gather.5
  335.9 51.7 reduce-scatter.3
  389.7 305.4 all-gather.7

commit v2 on v1

v2 whole, which is shorter than its diff:
```python
import jax
import jax.numpy as jnp
from jax import lax
from jax.experimental import pallas as pl
from jax.experimental.pallas import tpu as pltpu
from jax.sharding import PartitionSpec as P

HIGH = lax.Precision.HIGH
HIGHEST = lax.Precision.HIGHEST
STEP = 32
LANES = 128


def invert(permutation):
    block_ids = jnp.arange(permutation.shape[0], dtype=jnp.int32)
    hits = permutation[None, :] == block_ids[:, None]
    return jnp.sum(jnp.where(hits, block_ids[None, :], 0), axis=1).astype(jnp.int32)


def factor_kernel(diag_ref, upper_ref, inverse_ref, work_ref):
    size = diag_ref.shape[0]
    work_ref[:, :size] = diag_ref[...]
    rows = lax.broadcasted_iota(jnp.int32, (size, size), 0)
    lanes = lax.broadcasted_iota(jnp.int32, (size, size), 1)
    work_ref[:, size:] = jnp.where(rows == lanes, 1.0, 0.0)
    row_ids = lax.broadcasted_iota(jnp.int32, (STEP, LANES), 0)
    lane_ids = lax.broadcasted_iota(jnp.int32, (STEP, LANES), 1)
    for start in range(0, size, STEP):
        base = start // LANES * LANES
        tile = work_ref[start : start + STEP, base : base + LANES]
        unit = jnp.where(row_ids == lane_ids, 1.0, 0.0)
        pivots = jnp.ones((STEP, LANES), jnp.float32)
        for k in range(STEP):
            lane = start - base + k
            column = jnp.broadcast_to(tile[:, lane : lane + 1], (STEP, LANES))
            pivot = jnp.broadcast_to(column[k : k + 1, :], (STEP, LANES))
            pivots = jnp.where(row_ids == k, pivot, pivots)
            if k < STEP - 1:
                scaled = jnp.where(row_ids > k, column / pivot, 0.0)
                tile = tile - scaled * tile[k : k + 1, :]
                unit = unit - scaled * unit[k : k + 1, :]
        small = (unit / jnp.sqrt(pivots))[:, :STEP]
        final = jnp.dot(
            small,
            work_ref[start : start + STEP, :],
            precision=HIGHEST,
            preferred_element_type=jnp.float32,
        )
        upper_ref[start : start + STEP, :] = final[:, :size]
        inverse_ref[start : start + STEP, :] = final[:, size:]
        if start + STEP < size:
            below = start + STEP
            update = lax.dot_general(
                final[:, below // LANES * LANES : size],
                final,
                (((0,), (0,)), ((), ())),
                precision=HIGHEST,
                preferred_element_type=jnp.float32,
            )
            skip = below - below // LANES * LANES
            work_ref[below:, :] = work_ref[below:, :] - update[skip:, :]


def factor(diag_block):
    size = diag_block.shape[0]
    shape = jax.ShapeDtypeStruct((size, size), jnp.float32)
    upper, inverse = pl.pallas_call(
        factor_kernel,
        out_shape=(shape, shape),
        scratch_shapes=[pltpu.VMEM((size, 2 * size), jnp.float32)],
        name="factor",
    )(diag_block)
    ids = jnp.arange(size, dtype=jnp.int32)
    lower = jnp.where(ids[:, None] >= ids[None, :], upper.T, 0.0)
    return lower, jnp.where(ids[:, None] >= ids[None, :], inverse, 0.0)


def make_panel(raw_column, pivot_block, alive_set):
    block_size = raw_column.shape[1]
    block_count = raw_column.shape[0] // block_size
    diag_block = lax.dynamic_slice_in_dim(raw_column, pivot_block * block_size, block_size, 0)
    lower, inverse = factor(diag_block)
    solved = jnp.dot(raw_column, inverse.T, precision=HIGHEST)
    block_ids = jnp.arange(block_count, dtype=jnp.int32)
    keep = (alive_set & (block_ids != pivot_block))[:, None, None]
    tiles = solved.reshape(block_count, block_size, block_size)
    on_pivot = (block_ids == pivot_block)[:, None, None]
    tiles = jnp.where(on_pivot, lower[None], jnp.where(keep, tiles, 0.0))
    return tiles.reshape(block_count * block_size, block_size)


def halves(value):
    top = value.astype(jnp.bfloat16)
    return top, (value - top.astype(jnp.float32)).astype(jnp.bfloat16)


def outer(left, right):
    contract = (((1,), (1,)), ((), ()))
    left_top, left_low = halves(left)
    right_top, right_low = halves(right)
    dot = lambda a, b: lax.dot_general(a, b, contract, preferred_element_type=jnp.float32)
    return dot(left_top, right_top) + (dot(left_top, right_low) + dot(left_low, right_top))


def update_kernel(
    flags, place, front_ref, first_ref, second_ref, own_first_ref, own_second_ref, out_ref, send_ref
):
    tile = pl.program_id(0)
    first, second, mine = flags[0], flags[1], flags[2]
    tile_first, tile_second = first_ref[...], second_ref[...]
    product = outer(tile_first, own_first_ref[...]) + outer(tile_second, own_second_ref[...])
    dead_row = (tile == first) | (tile == second)
    updated = jnp.where(dead_row, 0.0, front_ref[...] - product)
    out_ref[...] = jnp.where(
        mine == first, tile_first, jnp.where(mine == second, tile_second, updated)
    )
    dead_column = (mine == first) | (mine == second)
    send_ref[0] = jnp.where(dead_column, 0.0, updated)


def update(front, panel_first, panel_second, flags, place):
    rows, size = front.shape
    count = rows // size
    mine = lambda i, flags, place: (i, 0)
    own = lambda i, flags, place: (flags[2], 0)
    block = (size, size)
    return pl.pallas_call(
        update_kernel,
        grid_spec=pltpu.PrefetchScalarGridSpec(
            num_scalar_prefetch=2,
            grid=(count,),
            in_specs=[pl.BlockSpec(block, mine)] * 3 + [pl.BlockSpec(block, own)] * 2,
            out_specs=[
                pl.BlockSpec(block, mine),
                pl.BlockSpec((1, size, size), lambda i, flags, place: (place[i], 0, 0)),
            ],
        ),
        out_shape=(
            jax.ShapeDtypeStruct((rows, size), jnp.float32),
            jax.ShapeDtypeStruct((count, size, size), jnp.float32),
        ),
        name="update",
    )(flags, place, front, panel_first, panel_second, panel_first, panel_second)


def place_kernel(source, tile_ref, out_ref):
    out_ref[...] = tile_ref[0]


def place_tiles(tiles, inverse):
    count, size, _ = tiles.shape
    return pl.pallas_call(
        place_kernel,
        grid_spec=pltpu.PrefetchScalarGridSpec(
            num_scalar_prefetch=1,
            grid=(count,),
            in_specs=[pl.BlockSpec((1, size, size), lambda b, source: (source[b], 0, 0))],
            out_specs=pl.BlockSpec((size, size), lambda b, source: (0, b)),
        ),
        out_shape=jax.ShapeDtypeStruct((size, count * size), jnp.float32),
        name="place",
    )(inverse, tiles)


def block_row(tiles, pivot_block):
    return lax.dynamic_index_in_dim(tiles, pivot_block, 0, keepdims=False)


def shards(leaf_fronts, root_front, leaf_order, leaf_map, root_order):
    order_rows, block_size = leaf_fronts.shape
    block_count = order_rows // block_size
    my_block = lax.axis_index("front").astype(jnp.int32)
    leaf_index = lax.axis_index("leaf")
    slice_width = root_front.shape[2]
    block_ids = jnp.arange(block_count, dtype=jnp.int32)
    own_start = my_block * block_size

    tiles = leaf_fronts.reshape(block_count, block_size, block_size)
    first, second = leaf_order[0, 0], leaf_order[0, 1]
    raw_first = lax.all_gather(block_row(tiles, first).T, "front", axis=0, tiled=True)
    raw_second = lax.all_gather(block_row(tiles, second).T, "front", axis=0, tiled=True)
    everything = jnp.ones((block_count,), dtype=jnp.bool_)
    panel_first = make_panel(raw_first, first, everything)
    raw_second, root_rows = lax.optimization_barrier((raw_second, root_front[:, 0, :].T))
    pivot_rows = lax.dynamic_slice_in_dim(panel_first, second * block_size, block_size, 0)
    raw_second = raw_second - jnp.dot(panel_first, pivot_rows.T, precision=HIGH)
    panel_second = make_panel(raw_second, second, block_ids != first)

    flags = jnp.stack([first, second, my_block])
    leaf_out, outgoing = update(leaf_fronts, panel_first, panel_second, flags, leaf_map[0])
    incoming = lax.all_to_all(outgoing, "front", split_axis=0, concat_axis=0, tiled=True)
    gathered = place_tiles(incoming, invert(leaf_map[0]))
    part = lax.psum_scatter(gathered, "leaf", scatter_dimension=0, tiled=True)
    part = part + root_rows

    pivot = root_order[0]
    row = lax.dynamic_slice_in_dim(part, pivot * block_size, block_size, 1)
    row = lax.all_gather(row, "leaf", axis=0, tiled=True)
    raw_root = lax.all_gather(row, "front", axis=0, tiled=True)
    panel = make_panel(raw_root, pivot, everything)
    own = lax.dynamic_slice_in_dim(panel, own_start + leaf_index * slice_width, slice_width, 0)
    part = part - jnp.dot(own, panel.T, precision=HIGH)
    part = part.reshape(slice_width, block_count, block_size)
    part = jnp.where((block_ids != pivot)[None, :, None], part, 0.0)
    part = part.reshape(slice_width, order_rows)
    own_panel = lax.dynamic_slice_in_dim(panel, leaf_index * slice_width, slice_width, 1)
    root_out = jnp.where(my_block == pivot, own_panel, part.T)
    return (leaf_out, root_out[:, None, :])


def solution(mesh):
    return jax.shard_map(
        shards,
        mesh=mesh,
        in_specs=(
            P("leaf", "front"),
            P(None, "front", "leaf"),
            P("leaf", None),
            P("leaf", None),
            P(),
        ),
        out_specs=(P("leaf", "front"), P(None, "front", "leaf")),
        check_vma=False,
    )
```

time: 792 us -> 496 us (0.63)
  other arithmetic: 187 us -> 5.78 us
  waiting for transfers between devices: 403 us -> 227 us
  Pallas kernels: 0 us -> 142 us
  local copies, waits for them, and re-layouts: 72.4 us -> 39 us
  blocking collectives: 54.1 us -> 24.3 us
  matrix products: 40.5 us -> 25 us
    all_gather x1, waiting for transfers between devices: 300 us -> 61.1 us  [shards(): raw_root = lax.all_gather(row, 'front', axis=0, tiled=True)]
    another operation x27 -> x1, other arithmetic: 163 us -> 1.98 us  [shards(): flags = jnp.stack([first, second, my_block])]
    pallas_call x0 -> x5, Pallas kernels: none -> 142 us  [the longest x3 114 us: factor(): pl.pallas_call(factor_kernel, out_shape=(shape, shape), scratch_shapes=[p...]
    all_to_all x1 -> x0, blocking collectives: 54.1 us -> none  [shards(): lax.all_to_all(outgoing, 'front', split_axis=0, concat_axis=0, tiled=True)]
    all_to_all x0 -> x1, waiting for transfers between devices: none -> 52.1 us  [shards(): lax.all_to_all(outgoing, 'front', split_axis=0, concat_axis=0, tiled=True)]
    all_gather x0 -> x1, blocking collectives: none -> 24.3 us  [shards(): row = lax.all_gather(row, 'leaf', axis=0, tiled=True)]
    another operation x15 -> x0, matrix products: 24.2 us -> none  [the longest x9 22.8 us: make_panel(): lax.linalg.triangular_solve(lower, raw_column, left_side=False, lower=Tru...]
    unnamed x25, local copies, waits for them, and re-layouts: 31.1 us -> 16.1 us
  transfers between devices with their start and end apart: 4 -> 5, of which waited for: 3 -> 5; matrix products, arithmetic and copies ran while one was open for 11% -> 5% of each run, Pallas kernels for 0% -> 8%
where the time goes in v2:
time: 496 us; the launch traced here: 487 us
  waiting for transfers between devices  227 us (46%)
  Pallas kernels  142 us (29%)
  local copies, waits for them, and re-layouts  39 us (8%)
  matrix products  25 us (5%)
  blocking collectives  24.3 us (5%)
  between operations  19.9 us (4%)
  other arithmetic  5.78 us (1%)
    pallas_call x3, Pallas kernels, factor(): pl.pallas_call(factor_kernel, out_shape=(shape, shape), scratch_shapes=[p...  114 us
    all_gather x1, waiting for transfers between devices, shards(): raw_root = lax.all_gather(row, 'front', axis=0, tiled=True)  61.1 us
    reduce_scatter x1, waiting for transfers between devices, shards(): part = lax.psum_scatter(gathered, 'leaf', scatter_dimension=0, tiled=True)  59.6 us
    all_gather x1, waiting for transfers between devices, shards(): lax.all_gather(block_row(tiles, first).T, 'front', axis=0, tiled=True)  53.1 us
    all_to_all x1, waiting for transfers between devices, shards(): lax.all_to_all(outgoing, 'front', split_axis=0, concat_axis=0, tiled=True)  52.1 us
    all_gather x1, blocking collectives, shards(): row = lax.all_gather(row, 'leaf', axis=0, tiled=True)  24.3 us
    pallas_call x1, Pallas kernels, update(): pl.pallas_call(update_kernel, grid_spec=pltpu.PrefetchScalarGridSpec(num_...  16.4 us
    unnamed x25, local copies, waits for them, and re-layouts  16.1 us
  transfers between devices with their start and end apart: 5, of which 5 were waited for; matrix products, arithmetic and copies ran while one was open for 5% of the time, Pallas kernels for 8%

profile of v2, /device:TPU:1, one launch (start us, length us, event | category | flops | bytes accessed | tf_op | source)
XLA Modules:
  0.0 487.2 jit_solution(17954889383541706778)
XLA Ops:
  7.2 1.4 fusion.20
  12.6 1.1 constant_dynamic-slice_fusion.3
  13.6 0.8 copy.40
  14.5 0.9 copy.41
  16.8 0.7 iota_compare_fusion.8
  17.4 0.1 broadcast_in_dim.156
  17.5 0.1 broadcast_in_dim.150
  17.6 1.3 compare_and_fusion
  18.9 0.1 broadcast_in_dim.165
  19.1 2.0 pad_add_fusion.flags
  21.1 53.1 %all-gather.4.cloned.1.call-done = f32[4096,256]{1,0:T(8,128)} async-done(((f32[256,256]{1,0:T(8,128)}), f32[4096,256]{1,0:T(8,128)}) %all-gather.4.cloned.1.call-update) | async-done | bytes 4194320 | tf_op jit(solution)/shard_map/all_gather | solution.py:180
  74.3 1.7 constant_dynamic-slice_fusion.4.diag_ref
  75.9 38.1 %factor.3 = (f32[256,256]{1,0:T(8,128)}, f32[256,256]{1,0:T(8,128)}) custom-call(f32[256,256]{1,0:T(8,128)} %constant_dynamic-slice_fusion.4.diag_ref), custom_call_target="tpu_custom_call" | custom-call | tf_op jit(solution)/shard_map/factor/pallas_call | solution.py:67
  114.0 1.1 copy.23
  115.1 0.1 copy.24
  115.2 0.3 broadcast_in_dim.154
  115.6 3.9 copy.42
  119.5 5.7 %fusion = f32[4096,256]{0,1:T(8,128)} fusion(f32[4096,256]{0,1:T(8,128)S(1)} %bitcast.52, f32[4096,256]{1,0:T(8,128)S(1)} %copy-done.2, pred[4096]{0:T(1024)(128)(4,1)S(1)} %broadcast_in_dim.157, pred[4096]{0:T(1024)(128)(4,1)S(1)} %broadcast_in_dim.151, f32[256,256]{1,0:T(8,128)S(1)} %copy-done.5), kind=kOutput, calls=%fused_computation.4 | convolution fusion | flops 3223453696 | bytes 12853248 | tf_op jit(solution)/shard_map/dot_general | solution.py:83
  125.2 5.6 %copy.30.first_ref.own_first_ref = f32[4096,256]{1,0:T(8,128)} copy(f32[4096,256]{0,1:T(8,128)} %fusion) | data formatting | bytes 8388608 | tf_op jit(solution)/shard_map/jit(_where)/select_n | solution.py:88
  130.9 0.9 all-gather.6.cloned.1.call-done
  131.7 7.0 %convolution_subtract_fusion = f32[4096,256]{1,0:T(8,128)S(1)} fusion(f32[4096,256]{1,0:T(8,128)} %all-gather.6.cloned.1.call-done, f32[4096,256]{0,1:T(8,128)} %fusion, s32[]{:T(128)S(6)} %select_n.93), kind=kOutput, calls=%fused_computation.3 | convolution fusion | flops 1611661312 | bytes 12845060 | tf_op jit(solution)/shard_map/dot_general | solution.py:186
  138.7 2.0 copy-done
  140.7 0.7 constant_dynamic-slice_fusion.2.diag_ref
  141.5 38.1 %factor.4 = (f32[256,256]{1,0:T(8,128)}, f32[256,256]{1,0:T(8,128)}) custom-call(f32[256,256]{1,0:T(8,128)} %constant_dynamic-slice_fusion.2.diag_ref), custom_call_target="tpu_custom_call" | custom-call | tf_op jit(solution)/shard_map/factor/pallas_call | solution.py:67
  179.5 1.1 copy.27
  180.6 0.1 copy.28
  180.8 0.3 broadcast_in_dim.163
  181.1 4.1 copy.43
  185.2 5.6 %fusion.1 = f32[4096,256]{0,1:T(8,128)} fusion(f32[4096,256]{0,1:T(8,128)S(1)} %bitcast.53, f32[4096,256]{1,0:T(8,128)S(1)} %copy-done.1, pred[4096]{0:T(1024)(128)(4,1)S(1)} %broadcast_in_dim.166, pred[4096]{0:T(1024)(128)(4,1)S(1)} %broadcast_in_dim.161, f32[256,256]{1,0:T(8,128)S(1)} %copy-done.6), kind=kOutput, calls=%fused_computation.5 | convolution fusion | flops 3223453696 | bytes 12853248 | tf_op jit(solution)/shard_map/dot_general | solution.py:83
  190.8 5.6 %copy.31.second_ref.own_second_ref = f32[4096,256]{1,0:T(8,128)} copy(f32[4096,256]{0,1:T(8,128)} %fusion.1) | data formatting | bytes 8388608 | tf_op jit(solution)/shard_map/jit(_where)/select_n | solution.py:88
  196.4 16.4 %update.1 = (f32[4096,256]{1,0:T(8,128)}, f32[16,256,256]{2,1,0:T(8,128)}) custom-call(s32[3]{0:T(128)} %pad_add_fusion.flags, s32[16]{0:T(128)} %bitcast.59, f32[4096,256]{1,0:T(8,128)} %front_ref.1, f32[4096,256]{1,0:T(8,128)} %copy.30.first_ref.own_first_ref, f32[4096,256]{1,0:T(8,128)} %copy.31.second_ref.own_second_ref, ...), custom_call_target="tpu_custom_call" | custom-call | tf_op jit(solution)/shard_map/update/pallas_call | solution.py:127
  212.8 4.6 all-to-all-start
  217.5 0.6 select_reduce_fusion.source
  218.1 52.1 %all-to-all-done.tile_ref = f32[16,256,256]{2,1,0:T(8,128)} async-done(((f32[16,256,256]{2,1,0:T(8,128)}), f32[16,256,256]{2,1,0:T(8,128)}, u32[]{:S(2)}, u32[]{:S(2)}) %all-to-all-start) | async-done | bytes 4194336 | tf_op jit(solution)/shard_map/all_to_all | solution.py:191
  270.2 11.0 %place.1 = f32[256,4096]{1,0:T(8,128)} custom-call(s32[16]{0:T(128)} %select_reduce_fusion.source, f32[16,256,256]{2,1,0:T(8,128)} %all-to-all-done.tile_ref), custom_call_target="tpu_custom_call" | custom-call | tf_op jit(solution)/shard_map/place/pallas_call | solution.py:152
  281.3 0.6 copy-done.9
  281.9 59.6 %reduce-scatter.2.cloned.1.call-done = f32[32,4096]{1,0:T(8,128)} async-done(((f32[256,4096]{1,0:T(8,128)}), f32[32,4096]{1,0:T(8,128)}) %reduce-scatter.2.cloned.1.call-update) | async-done | bytes 524304 | tf_op jit(solution)/shard_map/reduce_scatter | solution.py:193
  341.5 1.1 add.36
  342.6 24.3 %all_gather.14 = f32[256,256]{1,0:T(8,128)} all-gather(f32[32,256]{1,0:T(8,128)S(1)} %constant_dynamic-slice_fusion.1), channel_id=1, replica_groups=mesh['leaf'=8,'front'=16] {'leaf'}, dimensions={0}, use_global_device_ids=true | all-gather | bytes 294912 | tf_op jit(solution)/shard_map/all_gather | solution.py:198
  367.2 61.1 %all-gather.8.cloned.1.call-done = f32[4096,256]{1,0:T(8,128)} async-done(((f32[256,256]{1,0:T(8,128)}), f32[4096,256]{1,0:T(8,128)}) %all-gather.8.cloned.1.call-update) | async-done | bytes 4194320 | tf_op jit(solution)/shard_map/all_gather | solution.py:199
  428.3 1.7 constant_dynamic-slice_fusion.diag_ref
  430.0 38.1 %factor.5 = (f32[256,256]{1,0:T(8,128)}, f32[256,256]{1,0:T(8,128)}) custom-call(f32[256,256]{1,0:T(8,128)} %constant_dynamic-slice_fusion.diag_ref), custom_call_target="tpu_custom_call" | custom-call | tf_op jit(solution)/shard_map/factor/pallas_call | solution.py:67
  468.1 1.1 copy.34
  469.2 0.1 copy.35
  469.3 0.3 broadcast_in_dim.173
  469.7 3.9 copy.44
  473.6 4.4 fusion.2
  478.0 2.2 fusion.6
  (40 shorter events, 0.7 us)
Async XLA Ops:
  7.2 67.1 %all-gather.4.cloned.1.call-start = ((), (), s32[]{:S(2)}) async-start(), calls=%async_computation.2 | async-start | bytes 4456448 | tf_op jit(solution)/shard_map/all_gather | solution.py:180
  14.5 117.2 %all-gather.6.cloned.1.call-start = ((), (), s32[]{:S(2)}) async-start(), calls=%async_computation.3 | async-start | bytes 4456448 | tf_op jit(solution)/shard_map/all_gather | solution.py:181
  115.6 3.9 copy-start.2
  115.6 3.9 copy-start.5
  138.7 2.0 copy-start
  181.1 4.1 copy-start.1
  181.1 4.1 copy-start.6
  212.8 4.7 copy-start.8
  212.8 57.4 %all-to-all-start = ((f32[16,256,256]{2,1,0:T(8,128)}), f32[16,256,256]{2,1,0:T(8,128)}, u32[]{:S(2)}, u32[]{:S(2)}) async-start(f32[16,256,256]{2,1,0:T(8,128)} %get-tuple-element.18), calls=%async_computation | async-start | bytes 8388608 | tf_op jit(solution)/shard_map/all_to_all | solution.py:191
  217.5 124.1 %reduce-scatter.2.cloned.1.call-start = ((), (), s32[]{:S(2)}) async-start(), calls=%async_computation.4 | async-start | bytes 4718592 | tf_op jit(solution)/shard_map/reduce_scatter | solution.py:193
  281.2 0.7 copy-start.9
  281.2 60.3 %copy-start.4 = (f32[4096,1,32]{0,2,1:T(8,128)S(1)}, f32[4096,1,32]{0,2,1:T(8,128)}, u32[]{:S(2)}) copy-start(f32[4096,1,32]{0,2,1:T(8,128)} %param.6) | copy-start | bytes 1572868
  281.2 147.1 %all-gather.8.cloned.1.call-start = ((), (), s32[]{:S(2)}) async-start(), calls=%async_computation.5 | async-start | bytes 4456448 | tf_op jit(solution)/shard_map/all_gather | solution.py:199
  469.7 3.9 copy-start.3
  469.7 3.9 copy-start.7
Sparse Core Ops, SparseCore 0:
  14.6 59.5 all-gather.3
  76.7 55.0 all-gather.5
  281.3 60.1 reduce-scatter.1
  367.1 61.2 all-gather.7

commit v3 on v2

--- a/solution.py
+++ b/solution.py
@@ -8,6 +8,7 @@
 HIGH = lax.Precision.HIGH
 HIGHEST = lax.Precision.HIGHEST
 STEP = 32
+GROUP = 8
 LANES = 128
 
 
@@ -17,9 +18,9 @@
     return jnp.sum(jnp.where(hits, block_ids[None, :], 0), axis=1).astype(jnp.int32)
 
 
-def factor_kernel(diag_ref, upper_ref, inverse_ref, work_ref):
-    size = diag_ref.shape[0]
-    work_ref[:, :size] = diag_ref[...]
+def factor(diag, work_ref, upper_ref, inverse_ref):
+    size = diag.shape[0]
+    work_ref[:, :size] = diag
     rows = lax.broadcasted_iota(jnp.int32, (size, size), 0)
     lanes = lax.broadcasted_iota(jnp.int32, (size, size), 1)
     work_ref[:, size:] = jnp.where(rows == lanes, 1.0, 0.0)
@@ -29,17 +30,25 @@
         base = start // LANES * LANES
         tile = work_ref[start : start + STEP, base : base + LANES]
         unit = jnp.where(row_ids == lane_ids, 1.0, 0.0)
-        pivots = jnp.ones((STEP, LANES), jnp.float32)
-        for k in range(STEP):
-            lane = start - base + k
-            column = jnp.broadcast_to(tile[:, lane : lane + 1], (STEP, LANES))
-            pivot = jnp.broadcast_to(column[k : k + 1, :], (STEP, LANES))
-            pivots = jnp.where(row_ids == k, pivot, pivots)
-            if k < STEP - 1:
-                scaled = jnp.where(row_ids > k, column / pivot, 0.0)
-                tile = tile - scaled * tile[k : k + 1, :]
-                unit = unit - scaled * unit[k : k + 1, :]
-        small = (unit / jnp.sqrt(pivots))[:, :STEP]
+        roots = jnp.ones((STEP, LANES), jnp.float32)
+        for group in range(0, STEP, GROUP):
+            lane = start - base + group
+            columns = [
+                jnp.broadcast_to(tile[:, lane + k : lane + k + 1], (STEP, LANES))
+                for k in range(GROUP)
+            ]
+            for k in range(GROUP):
+                row = group + k
+                pivot = columns[k][row : row + 1, :]
+                roots = jnp.where(row_ids == row, pivot, roots)
+                if row == STEP - 1:
+                    break
+                scaled = jnp.where(row_ids > row, columns[k] * (1.0 / pivot), 0.0)
+                for later in range(k + 1, GROUP):
+                    columns[later] = columns[later] - scaled * columns[later][row : row + 1, :]
+                tile = tile - scaled * tile[row : row + 1, :]
+                unit = unit - scaled * unit[row : row + 1, :]
+        small = (unit / jnp.sqrt(roots))[:, :STEP]
         final = jnp.dot(
             small,
             work_ref[start : start + STEP, :],
@@ -59,34 +68,68 @@
             )
             skip = below - below // LANES * LANES
             work_ref[below:, :] = work_ref[below:, :] - update[skip:, :]
-
-
-def factor(diag_block):
-    size = diag_block.shape[0]
-    shape = jax.ShapeDtypeStruct((size, size), jnp.float32)
-    upper, inverse = pl.pallas_call(
-        factor_kernel,
-        out_shape=(shape, shape),
-        scratch_shapes=[pltpu.VMEM((size, 2 * size), jnp.float32)],
-        name="factor",
-    )(diag_block)
-    ids = jnp.arange(size, dtype=jnp.int32)
-    lower = jnp.where(ids[:, None] >= ids[None, :], upper.T, 0.0)
-    return lower, jnp.where(ids[:, None] >= ids[None, :], inverse, 0.0)
-
-
-def make_panel(raw_column, pivot_block, alive_set):
-    block_size = raw_column.shape[1]
-    block_count = raw_column.shape[0] // block_size
-    diag_block = lax.dynamic_slice_in_dim(raw_column, pivot_block * block_size, block_size, 0)
-    lower, inverse = factor(diag_block)
-    solved = jnp.dot(raw_column, inverse.T, precision=HIGHEST)
-    block_ids = jnp.arange(block_count, dtype=jnp.int32)
-    keep = (alive_set & (block_ids != pivot_block))[:, None, None]
-    tiles = solved.reshape(block_count, block_size, block_size)
-    on_pivot = (block_ids == pivot_block)[:, None, None]
-    tiles = jnp.where(on_pivot, lower[None], jnp.where(keep, tiles, 0.0))
-    return tiles.reshape(block_count * block_size, block_size)
+    lower = jnp.where(rows >= lanes, upper_ref[...].T, 0.0)
+    inverse_t = jnp.where(rows <= lanes, inverse_ref[...].T, 0.0)
+    return lower, inverse_t
+
+
+def panel_kernel(pivot, keep, raw_ref, diag_ref, *rest):
+    before, (out_ref, work_ref, lower_ref, inverse_ref, before_ref) = rest[:-5], rest[-5:]
+    step = pl.program_id(0)
+
+    @pl.when(step == 0)
+    def _():
+        diag = diag_ref[...]
+        if before:
+            pivot_rows = before[1][...]
+            before_ref[...] = pivot_rows.T
+            diag = diag - jnp.dot(
+                pivot_rows,
+                before_ref[...],
+                precision=HIGHEST,
+                preferred_element_type=jnp.float32,
+            )
+        lower, inverse_t = factor(diag, work_ref, lower_ref, inverse_ref)
+        lower_ref[...] = lower
+        inverse_ref[...] = inverse_t
+
+    @pl.when(step > 0)
+    def _():
+        tile = step - 1
+        raw = raw_ref[...]
+        if before:
+            raw = raw - product(before[0][...], before_ref[...])
+        solved = jnp.dot(
+            raw, inverse_ref[...], precision=HIGHEST, preferred_element_type=jnp.float32
+        )
+        solved = jnp.where(keep[tile] != 0, solved, 0.0)
+        out_ref[...] = jnp.where(tile == pivot[0], lower_ref[...], solved)
+
+
+def make_panel(raw_column, pivot_block, alive_set, before=None):
+    rows, size = raw_column.shape
+    count = rows // size
+    block = (size, size)
+    tile = pl.BlockSpec(block, lambda s, pivot, keep: (jnp.maximum(s - 1, 0), 0))
+    fixed = pl.BlockSpec(block, lambda s, pivot, keep: (pivot[0], 0))
+    extra = () if before is None else (before, before)
+    return pl.pallas_call(
+        panel_kernel,
+        grid_spec=pltpu.PrefetchScalarGridSpec(
+            num_scalar_prefetch=2,
+            grid=(count + 1,),
+            in_specs=[tile, fixed] * (2 if extra else 1),
+            out_specs=tile,
+            scratch_shapes=[
+                pltpu.VMEM((size, 2 * size), jnp.float32),
+                pltpu.VMEM(block, jnp.float32),
+                pltpu.VMEM(block, jnp.float32),
+                pltpu.VMEM(block, jnp.float32),
+            ],
+        ),
+        out_shape=jax.ShapeDtypeStruct((rows, size), jnp.float32),
+        name="panel",
+    )(pivot_block[None], alive_set.astype(jnp.int32), raw_column, raw_column, *extra)
 
 
 def halves(value):
@@ -94,23 +137,36 @@
     return top, (value - top.astype(jnp.float32)).astype(jnp.bfloat16)
 
 
-def outer(left, right):
-    contract = (((1,), (1,)), ((), ()))
-    left_top, left_low = halves(left)
-    right_top, right_low = halves(right)
-    dot = lambda a, b: lax.dot_general(a, b, contract, preferred_element_type=jnp.float32)
-    return dot(left_top, right_top) + (dot(left_top, right_low) + dot(left_low, right_top))
+def product(left, right):
+    return split_product(left, *halves(right))
+
+
+def split_product(left, right_top, right_low):
+    top, low = halves(left)
+    dot = lambda a, b: jnp.dot(a, b, preferred_element_type=jnp.float32)
+    return dot(top, right_top) + (dot(top, right_low) + dot(low, right_top))
 
 
 def update_kernel(
-    flags, place, front_ref, first_ref, second_ref, own_first_ref, own_second_ref, out_ref, send_ref
+    flags, place, front_ref, first_ref, second_ref, own_first_ref, own_second_ref,
+    out_ref, send_ref, top_ref, low_ref,
 ):
     tile = pl.program_id(0)
     first, second, mine = flags[0], flags[1], flags[2]
+
+    @pl.when(tile == 0)
+    def _():
+        for slot, own in enumerate((own_first_ref, own_second_ref)):
+            top, low = halves(own[...].T)
+            top_ref[slot] = top
+            low_ref[slot] = low
+
     tile_first, tile_second = first_ref[...], second_ref[...]
-    product = outer(tile_first, own_first_ref[...]) + outer(tile_second, own_second_ref[...])
+    total = split_product(tile_first, top_ref[0], low_ref[0]) + split_product(
+        tile_second, top_ref[1], low_ref[1]
+    )
     dead_row = (tile == first) | (tile == second)
-    updated = jnp.where(dead_row, 0.0, front_ref[...] - product)
+    updated = jnp.where(dead_row, 0.0, front_ref[...] - total)
     out_ref[...] = jnp.where(
         mine == first, tile_first, jnp.where(mine == second, tile_second, updated)
     )
@@ -134,6 +190,7 @@
                 pl.BlockSpec(block, mine),
                 pl.BlockSpec((1, size, size), lambda i, flags, place: (place[i], 0, 0)),
             ],
+            scratch_shapes=[pltpu.VMEM((2, size, size), jnp.bfloat16)] * 2,
         ),
         out_shape=(
             jax.ShapeDtypeStruct((rows, size), jnp.float32),
@@ -179,24 +236,41 @@
     first, second = leaf_order[0, 0], leaf_order[0, 1]
     raw_first = lax.all_gather(block_row(tiles, first).T, "front", axis=0, tiled=True)
     raw_second = lax.all_gather(block_row(tiles, second).T, "front", axis=0, tiled=True)
+    inverse = invert(leaf_map[0])
+    pivot = root_order[0]
+    source = inverse[pivot]
+    raw_source = lax.all_gather(block_row(tiles, source).T, "front", axis=0, tiled=True)
     everything = jnp.ones((block_count,), dtype=jnp.bool_)
     panel_first = make_panel(raw_first, first, everything)
-    raw_second, root_rows = lax.optimization_barrier((raw_second, root_front[:, 0, :].T))
-    pivot_rows = lax.dynamic_slice_in_dim(panel_first, second * block_size, block_size, 0)
-    raw_second = raw_second - jnp.dot(panel_first, pivot_rows.T, precision=HIGH)
-    panel_second = make_panel(raw_second, second, block_ids != first)
+    root_rows = root_front[:, 0, :].T
+    raw_second, raw_source, root_rows = lax.optimization_barrier(
+        (raw_second, raw_source, root_rows)
+    )
+    panel_second = make_panel(raw_second, second, block_ids != first, panel_first)
+
+    into = inverse[my_block]
+    rows_of = lambda panel, block: lax.dynamic_slice_in_dim(
+        panel, block * block_size, block_size, 0
+    )
+    share = rows_of(raw_source, into)
+    for panel in (panel_first, panel_second):
+        share = share - jnp.dot(rows_of(panel, into), rows_of(panel, source).T, precision=HIGH)
+    live = (into != first) & (into != second) & (source != first) & (source != second)
+    share = jnp.where(live, share, 0.0)
+    root_share = lax.dynamic_slice_in_dim(root_rows, pivot * block_size, block_size, 1)
+    here = leaf_index * slice_width
+    widened = jnp.zeros_like(share)
+    widened = lax.dynamic_update_slice_in_dim(widened, root_share, here, 0)
+    raw_root = lax.psum(share + widened, "leaf")
+    raw_root = lax.all_gather(raw_root, "front", axis=0, tiled=True)
 
     flags = jnp.stack([first, second, my_block])
     leaf_out, outgoing = update(leaf_fronts, panel_first, panel_second, flags, leaf_map[0])
     incoming = lax.all_to_all(outgoing, "front", split_axis=0, concat_axis=0, tiled=True)
-    gathered = place_tiles(incoming, invert(leaf_map[0]))
+    gathered = place_tiles(incoming, inverse)
     part = lax.psum_scatter(gathered, "leaf", scatter_dimension=0, tiled=True)
     part = part + root_rows
 
-    pivot = root_order[0]
-    row = lax.dynamic_slice_in_dim(part, pivot * block_size, block_size, 1)
-    row = lax.all_gather(row, "leaf", axis=0, tiled=True)
-    raw_root = lax.all_gather(row, "front", axis=0, tiled=True)
     panel = make_panel(raw_root, pivot, everything)
     own = lax.dynamic_slice_in_dim(panel, own_start + leaf_index * slice_width, slice_width, 0)
     part = part - jnp.dot(own, panel.T, precision=HIGH)

time: 496 us -> 489 us (0.986); the launches traced: 487 us -> 487 us
  blocking collectives: 24.3 us -> 69.3 us
  Pallas kernels: 142 us -> 109 us
  waiting for transfers between devices: 227 us -> 258 us
  local copies, waits for them, and re-layouts: 39 us -> 10.4 us
  matrix products: 25 us -> 7.84 us
  between operations: 19.9 us -> 28.6 us
    all_to_all x0 -> x1, blocking collectives: none -> 69.3 us  [shards(): lax.all_to_all(outgoing, 'front', split_axis=0, concat_axis=0, tiled=True)]
    psum x0 -> x1, waiting for transfers between devices: none -> 67.7 us  [shards(): raw_root = lax.psum(share + widened, 'leaf')]
    all_gather x1, waiting for transfers between devices: 0.87 us -> 57.8 us  [shards(): lax.all_gather(block_row(tiles, second).T, 'front', axis=0, tiled=True)]
    all_to_all x1 -> x0, waiting for transfers between devices: 52.1 us -> none  [shards(): lax.all_to_all(outgoing, 'front', split_axis=0, concat_axis=0, tiled=True)]
    reduce_scatter x1, waiting for transfers between devices: 59.6 us -> 23.7 us  [shards(): part = lax.psum_scatter(gathered, 'leaf', scatter_dimension=0, tiled=True)]
    pallas_call x3, Pallas kernels: 114 us -> 81.4 us  [make_panel(): pl.pallas_call(panel_kernel, grid_spec=pltpu.PrefetchScalarGridSpec(num_s...]
    all_gather x1 -> x0, blocking collectives: 24.3 us -> none  [shards(): row = lax.all_gather(row, 'leaf', axis=0, tiled=True)]
    dot_general x4 -> x2, matrix products: 22.7 us -> 2.83 us  [shards(): jnp.dot(rows_of(panel, into), rows_of(panel, source).T, precision=HIGH)]
  transfers between devices with their start and end apart: 5 -> 6, of which waited for: 5 -> 6; matrix products, arithmetic and copies ran while one was open for 5% -> 2% of each run, Pallas kernels for 8% -> 11%
where the time goes in v3:
time: 489 us; the launch traced here: 487 us
  waiting for transfers between devices  258 us (53%)
  Pallas kernels  109 us (22%)
  blocking collectives  69.3 us (14%)
  between operations  28.6 us (6%)
  local copies, waits for them, and re-layouts  10.4 us (2%)
  matrix products  7.84 us (2%)
    pallas_call x3, Pallas kernels, make_panel(): pl.pallas_call(panel_kernel, grid_spec=pltpu.PrefetchScalarGridSpec(num_s...  81.4 us
    all_to_all x1, blocking collectives, shards(): lax.all_to_all(outgoing, 'front', split_axis=0, concat_axis=0, tiled=True)  69.3 us
    psum x1, waiting for transfers between devices, shards(): raw_root = lax.psum(share + widened, 'leaf')  67.7 us
    all_gather x1, waiting for transfers between devices, shards(): lax.all_gather(block_row(tiles, first).T, 'front', axis=0, tiled=True)  57.8 us
    all_gather x1, waiting for transfers between devices, shards(): lax.all_gather(block_row(tiles, second).T, 'front', axis=0, tiled=True)  57.8 us
    all_gather x1, waiting for transfers between devices, shards(): lax.all_gather(block_row(tiles, source).T, 'front', axis=0, tiled=True)  49.8 us
    reduce_scatter x1, waiting for transfers between devices, shards(): part = lax.psum_scatter(gathered, 'leaf', scatter_dimension=0, tiled=True)  23.7 us
    pallas_call x1, Pallas kernels, update(): pl.pallas_call(update_kernel, grid_spec=pltpu.PrefetchScalarGridSpec(num_...  16.3 us
  transfers between devices with their start and end apart: 6, of which 6 were waited for; matrix products, arithmetic and copies ran while one was open for 2% of the time, Pallas kernels for 11%

profile of v3, /device:TPU:1, one launch (start us, length us, event | category | flops | bytes accessed | tf_op | source)
XLA Modules:
  0.0 486.9 jit_solution(8050308430615857824)
XLA Ops:
  7.2 0.0 all-gather.9.cloned.1.call-start
  8.5 0.8 select_reduce_fusion.source
  9.3 0.0 copy-start.2
  9.9 0.7 fusion.13
  12.0 1.3 fusion.14
  17.3 1.2 constant_dynamic-slice_fusion
  18.5 0.8 copy.17
  19.4 0.0 all-gather.9.cloned.1.call-update
  19.4 0.0 all-gather.7.cloned.1.call-start
  19.4 0.8 copy.16
  20.3 0.0 all-gather.7.cloned.1.call-update
  20.3 0.0 all-gather.5.cloned.1.call-start
  20.3 0.8 copy.15
  21.2 0.0 all-gather.5.cloned.1.call-update
  21.2 0.0 all-reduce.2.cloned.1.call-start
  28.2 1.1 compare_convert_fusion.keep
  29.4 49.8 %all-gather.9.cloned.1.call-done = f32[4096,256]{1,0:T(8,128)} async-done(((f32[256,256]{1,0:T(8,128)}), f32[4096,256]{1,0:T(8,128)}) %all-gather.9.cloned.1.call-update) | async-done | bytes 4194320 | tf_op jit(solution)/shard_map/all_gather | solution.py:242
  79.1 57.8 %all-gather.7.cloned.1.call-done.raw_ref.diag_ref = f32[4096,256]{1,0:T(8,128)} async-done(((f32[256,256]{1,0:T(8,128)}), f32[4096,256]{1,0:T(8,128)}) %all-gather.7.cloned.1.call-update) | async-done | bytes 4194320 | tf_op jit(solution)/shard_map/all_gather | solution.py:238
  137.0 57.8 %all-gather.5.cloned.1.call-done.raw_ref.diag_ref = f32[4096,256]{1,0:T(8,128)} async-done(((f32[256,256]{1,0:T(8,128)}), f32[4096,256]{1,0:T(8,128)}) %all-gather.5.cloned.1.call-update) | async-done | bytes 4194320 | tf_op jit(solution)/shard_map/all_gather | solution.py:237
  194.8 0.6 broadcast_1_keep.2.keep
  195.3 25.6 %panel.3.rest_0_.rest_1_.first_ref.own_first_ref = f32[4096,256]{1,0:T(8,128)} custom-call(s32[1]{0:T(128)} %bitcast.pivot, s32[16]{0:T(128)} %broadcast_1_keep.2.keep, f32[4096,256]{1,0:T(8,128)} %all-gather.5.cloned.1.call-done.raw_ref.diag_ref, f32[4096,256]{1,0:T(8,128)} %all-gather.5.cloned.1.call-done.raw_ref.diag_ref), custom_call_target="tpu_custom_call" | custom-call | tf_op jit(solution)/shard_map/panel/pallas_call | solution.py:116
  220.9 0.0 copy-done.2
  220.9 1.5 convolution_subtract_fusion.2
  222.4 0.0 copy-start.1
  222.4 30.2 %panel.4.second_ref.own_second_ref = f32[4096,256]{1,0:T(8,128)} custom-call(s32[1]{0:T(128)} %bitcast.1.pivot, s32[16]{0:T(128)} %compare_convert_fusion.keep, f32[4096,256]{1,0:T(8,128)} %all-gather.7.cloned.1.call-done.raw_ref.diag_ref, f32[4096,256]{1,0:T(8,128)} %all-gather.7.cloned.1.call-done.raw_ref.diag_ref, ...), custom_call_target="tpu_custom_call" | custom-call | tf_op jit(solution)/shard_map/panel/pallas_call | solution.py:116
  252.6 1.4 fusion.4
  253.9 0.0 copy-done.1
  254.0 0.0 copy-start
  254.0 0.7 copy-done
  254.7 0.0 all-reduce.2.cloned.1.call-update
  254.7 0.0 all-gather.11.cloned.1.call-start
  254.7 67.7 %all-reduce.2.cloned.1.call-done = f32[256,256]{1,0:T(8,128)} async-done(((f32[256,256]{1,0:T(8,128)}), f32[256,256]{1,0:T(8,128)}) %all-reduce.2.cloned.1.call-update) | async-done | bytes 262160 | tf_op jit(solution)/shard_map/psum | solution.py:264
  322.4 0.0 all-gather.11.cloned.1.call-update
  322.5 0.0 reduce-scatter.2.cloned.1.call-start
  322.5 1.7 pad_add_fusion.flags
  324.2 16.3 %update.1 = (f32[4096,256]{1,0:T(8,128)}, f32[16,256,256]{2,1,0:T(8,128)}) custom-call(s32[3]{0:T(128)} %pad_add_fusion.flags, s32[16]{0:T(128)} %bitcast.46, f32[4096,256]{1,0:T(8,128)} %front_ref.1, f32[4096,256]{1,0:T(8,128)} %panel.3.rest_0_.rest_1_.first_ref.own_first_ref, f32[4096,256]{1,0:T(8,128)} %panel.4.second_ref.own_second_ref, ...), custom_call_target="tpu_custom_call" | custom-call | tf_op jit(solution)/shard_map/update/pallas_call | solution.py:183
  340.5 69.3 %all_to_all.5.tile_ref = f32[16,256,256]{2,1,0:T(8,128)} all-to-all(f32[16,256,256]{2,1,0:T(8,128)} %get-tuple-element.11), channel_id=1, replica_groups=mesh['leaf'=8,'front'=16] {'front'}, dimensions={0} | all-to-all | bytes 8388608 | tf_op jit(solution)/shard_map/all_to_all | solution.py:269
  409.9 11.0 %place.1 = f32[256,4096]{1,0:T(8,128)} custom-call(s32[16]{0:T(128)} %copy-done.2, f32[16,256,256]{2,1,0:T(8,128)} %all_to_all.5.tile_ref), custom_call_target="tpu_custom_call" | custom-call | tf_op jit(solution)/shard_map/place/pallas_call | solution.py:209
  420.9 0.0 copy-start.3
  420.9 0.0 reduce-scatter.2.cloned.1.call-update
  420.9 0.6 copy-done.3
  421.6 0.1 broadcast_in_dim.42
  421.7 1.2 all-gather.11.cloned.1.call-done.raw_ref.diag_ref
  422.9 25.6 %panel.5 = f32[4096,256]{1,0:T(8,128)} custom-call(s32[1]{0:T(128)} %bitcast.42, s32[16]{0:T(128)} %broadcast_1_keep.2.keep, f32[4096,256]{1,0:T(8,128)} %all-gather.11.cloned.1.call-done.raw_ref.diag_ref, f32[4096,256]{1,0:T(8,128)} %all-gather.11.cloned.1.call-done.raw_ref.diag_ref), custom_call_target="tpu_custom_call" | custom-call | tf_op jit(solution)/shard_map/panel/pallas_call | solution.py:116
  448.5 2.2 constant_dynamic-slice_fusion.1
  450.8 0.6 copy.18
  451.3 23.7 %reduce-scatter.2.cloned.1.call-done = f32[32,4096]{1,0:T(8,128)} async-done(((f32[256,4096]{1,0:T(8,128)}), f32[32,4096]{1,0:T(8,128)}) %reduce-scatter.2.cloned.1.call-update) | async-done | bytes 524304 | tf_op jit(solution)/shard_map/reduce_scatter | solution.py:271
  475.0 5.0 %fusion.3 = f32[4096,1,32]{0,2,1:T(8,128)} fusion(f32[4096,32]{0,1:T(8,128)S(1)} %copy.18, f32[4096,256]{1,0:T(8,128)} %panel.5, f32[32,4096]{1,0:T(8,128)} %reduce-scatter.2.cloned.1.call-done, f32[32,4096]{1,0:T(8,128)S(1)} %bitcast.37, pred[4096]{0:T(1024)(128)(4,1)S(1)} %broadcast_in_dim.43, pred[]{:T(512)S(6)} %eq.19, s32[]{:T(128)S(6)} %select_n.76), kind=kOutput, calls=%fused_computation.4 | convolution fusion | flops 201850880 | bytes 6328325 | tf_op jit(solution)/shard_map/dot_general | solution.py:276
  (3 shorter events, 0.1 us)
Async XLA Ops:
  7.2 72.0 %all-gather.9.cloned.1.call-start = ((), (), s32[]{:S(2)}) async-start(), calls=%async_computation.4 | async-start | bytes 4456448 | tf_op jit(solution)/shard_map/all_gather | solution.py:242
  9.3 211.6 %copy-start.2 = (s32[16]{0:T(128)}, s32[16]{0:T(128)S(1)}, u32[]{:S(2)}) copy-start(s32[16]{0:T(128)S(1)} %select_reduce_fusion.source) | copy-start | bytes 196
  19.4 117.6 %all-gather.7.cloned.1.call-start = ((), (), s32[]{:S(2)}) async-start(), calls=%async_computation.3 | async-start | bytes 4456448 | tf_op jit(solution)/shard_map/all_gather | solution.py:238
  20.3 174.5 %all-gather.5.cloned.1.call-start = ((), (), s32[]{:S(2)}) async-start(), calls=%async_computation.2 | async-start | bytes 4456448 | tf_op jit(solution)/shard_map/all_gather | solution.py:237
  21.2 301.2 %all-reduce.2.cloned.1.call-start = ((), (), s32[]{:S(2)}) async-start(), calls=%async_computation.5 | async-start | bytes 524288 | tf_op jit(solution)/shard_map/psum | solution.py:264
  222.4 31.6 %copy-start.1 = (f32[4096,1,32]{0,2,1:T(8,128)S(1)}, f32[4096,1,32]{0,2,1:T(8,128)}, u32[]{:S(2)}) copy-start(f32[4096,1,32]{0,2,1:T(8,128)} %param.6) | copy-start | bytes 1572868
  254.0 0.7 copy-start
  254.7 168.2 %all-gather.11.cloned.1.call-start = ((), (), s32[]{:S(2)}) async-start(), calls=%async_computation.6 | async-start | bytes 4456448 | tf_op jit(solution)/shard_map/all_gather | solution.py:265
  322.5 152.5 %reduce-scatter.2.cloned.1.call-start = ((), (), s32[]{:S(2)}) async-start(), calls=%async_computation.7 | async-start | bytes 4718592 | tf_op jit(solution)/shard_map/reduce_scatter | solution.py:271
  420.9 0.7 copy-start.3
Sparse Core Ops, SparseCore 0:
  19.5 59.5 all-gather.8
  82.1 54.7 all-gather.6
  139.9 54.7 all-gather.4
  254.8 67.5 all-reduce.1
  325.0 97.8 all-gather.10
  425.3 49.6 reduce-scatter.1

commit v4 on v3

--- a/solution.py
+++ b/solution.py
@@ -129,6 +129,9 @@
         ),
         out_shape=jax.ShapeDtypeStruct((rows, size), jnp.float32),
         name="panel",
+        cost_estimate=pl.CostEstimate(
+            flops=24 * rows * size * size, bytes_accessed=64 * rows * size, transcendentals=0
+        ),
     )(pivot_block[None], alive_set.astype(jnp.int32), raw_column, raw_column, *extra)
 
 
@@ -197,6 +200,9 @@
             jax.ShapeDtypeStruct((count, size, size), jnp.float32),
         ),
         name="update",
+        cost_estimate=pl.CostEstimate(
+            flops=12 * rows * size * size, bytes_accessed=32 * rows * size, transcendentals=0
+        ),
     )(flags, place, front, panel_first, panel_second, panel_first, panel_second)
 
 
@@ -234,19 +240,27 @@
 
     tiles = leaf_fronts.reshape(block_count, block_size, block_size)
     first, second = leaf_order[0, 0], leaf_order[0, 1]
-    raw_first = lax.all_gather(block_row(tiles, first).T, "front", axis=0, tiled=True)
-    raw_second = lax.all_gather(block_row(tiles, second).T, "front", axis=0, tiled=True)
     inverse = invert(leaf_map[0])
     pivot = root_order[0]
     source = inverse[pivot]
-    raw_source = lax.all_gather(block_row(tiles, source).T, "front", axis=0, tiled=True)
+    row_first = block_row(tiles, first).T
+    row_second = block_row(tiles, second).T
+    row_source = block_row(tiles, source).T
+    raw_first = lax.all_gather(row_first, "front", axis=0, tiled=True)
+    raw_first, row_second = lax.optimization_barrier((raw_first, row_second))
+    raw_second = lax.all_gather(row_second, "front", axis=0, tiled=True)
     everything = jnp.ones((block_count,), dtype=jnp.bool_)
     panel_first = make_panel(raw_first, first, everything)
     root_rows = root_front[:, 0, :].T
-    raw_second, raw_source, root_rows = lax.optimization_barrier(
-        (raw_second, raw_source, root_rows)
-    )
+    raw_second, root_rows, row_source, panel_first = lax.optimization_barrier(
+        (raw_second, root_rows, row_source, panel_first)
+    )
+    raw_source = lax.all_gather(row_source, "front", axis=0, tiled=True)
     panel_second = make_panel(raw_second, second, block_ids != first, panel_first)
+
+    flags = jnp.stack([first, second, my_block])
+    leaf_out, outgoing = update(leaf_fronts, panel_first, panel_second, flags, leaf_map[0])
+    raw_source, outgoing = lax.optimization_barrier((raw_source, outgoing))
 
     into = inverse[my_block]
     rows_of = lambda panel, block: lax.dynamic_slice_in_dim(
@@ -261,13 +275,13 @@
     here = leaf_index * slice_width
     widened = jnp.zeros_like(share)
     widened = lax.dynamic_update_slice_in_dim(widened, root_share, here, 0)
-    raw_root = lax.psum(share + widened, "leaf")
+    shares = lax.all_gather(share + widened, "leaf", axis=0)
+    raw_root = jnp.sum(shares, axis=0)
     raw_root = lax.all_gather(raw_root, "front", axis=0, tiled=True)
 
-    flags = jnp.stack([first, second, my_block])
-    leaf_out, outgoing = update(leaf_fronts, panel_first, panel_second, flags, leaf_map[0])
     incoming = lax.all_to_all(outgoing, "front", split_axis=0, concat_axis=0, tiled=True)
     gathered = place_tiles(incoming, inverse)
+    gathered, raw_root = lax.optimization_barrier((gathered, raw_root))
     part = lax.psum_scatter(gathered, "leaf", scatter_dimension=0, tiled=True)
     part = part + root_rows
 

time: 489 us -> 398 us (0.81)
  waiting for transfers between devices: 258 us -> 158 us
  local copies, waits for them, and re-layouts: 10.4 us -> 15.6 us
    psum x1 -> x0, waiting for transfers between devices: 67.7 us -> none  [shards(): raw_root = lax.psum(share + widened, 'leaf')]
    all_gather x3 -> x4, waiting for transfers between devices: 165 us -> 128 us  [the longest x1 58.9 us: shards(): raw_first = lax.all_gather(row_first, 'front', axis=0, tiled=True)]
    unnamed x6 -> x7, waiting for transfers between devices: 0.1 us -> 25.7 us
    reduce_scatter x1 -> x0, waiting for transfers between devices: 23.7 us -> none  [shards(): part = lax.psum_scatter(gathered, 'leaf', scatter_dimension=0, tiled=True)]
  transfers between devices with their start and end apart: 6 -> 6, of which waited for: 6 -> 6; matrix products, arithmetic and copies ran while one was open for 2% -> 2% of each run, Pallas kernels for 11% -> 27%
where the time goes in v4:
time: 398 us; the launch traced here: 395 us
  waiting for transfers between devices  158 us (40%)
  Pallas kernels  109 us (27%)
  blocking collectives  70.9 us (18%)
  between operations  27.4 us (7%)
  local copies, waits for them, and re-layouts  15.6 us (4%)
  matrix products  8.25 us (2%)
  other arithmetic  6.23 us (2%)
    pallas_call x3, Pallas kernels, make_panel(): pl.pallas_call(panel_kernel, grid_spec=pltpu.PrefetchScalarGridSpec(num_s...  81.2 us
    all_to_all x1, blocking collectives, shards(): lax.all_to_all(outgoing, 'front', split_axis=0, concat_axis=0, tiled=True)  70.9 us
    all_gather x1, waiting for transfers between devices, shards(): raw_first = lax.all_gather(row_first, 'front', axis=0, tiled=True)  58.9 us
    all_gather x1, waiting for transfers between devices, shards(): shares = lax.all_gather(share + widened, 'leaf', axis=0)  34.5 us
    all_gather x1, waiting for transfers between devices, shards(): raw_second = lax.all_gather(row_second, 'front', axis=0, tiled=True)  29.7 us
    unnamed x7, waiting for transfers between devices  25.7 us
    pallas_call x1, Pallas kernels, update(): pl.pallas_call(update_kernel, grid_spec=pltpu.PrefetchScalarGridSpec(num_...  16.3 us
    pallas_call x1, Pallas kernels, place_tiles(): pl.pallas_call(place_kernel, grid_spec=pltpu.PrefetchScalarGridSpec(num_s...  11 us
  transfers between devices with their start and end apart: 6, of which 6 were waited for; matrix products, arithmetic and copies ran while one was open for 2% of the time, Pallas kernels for 27%

profile of v4, /device:TPU:1, one launch (start us, length us, event | category | flops | bytes accessed | tf_op | source)
XLA Modules:
  0.0 395.4 jit_solution(2344777856232690076)
XLA Ops:
  7.2 0.0 all-gather.6.cloned.1.call-start
  8.5 0.8 select_reduce_fusion.source
  9.3 0.0 copy-start
  9.9 0.6 fusion.13
  11.8 1.3 fusion.14
  17.2 1.9 dynamic-slice_bitcast_fusion
  19.0 0.8 copy.26
  19.9 0.0 all-gather.6.cloned.1.call-update
  19.9 0.0 all-gather.8.cloned.1.call-start
  19.9 0.8 copy.27
  20.8 58.9 %all-gather.6.cloned.1.call-done.raw_ref.diag_ref = f32[4096,256]{1,0:T(8,128)} async-done(((f32[256,256]{1,0:T(8,128)}), f32[4096,256]{1,0:T(8,128)}) %all-gather.6.cloned.1.call-update) | async-done | bytes 4194320 | tf_op jit(solution)/shard_map/all_gather | solution.py:249
  79.6 0.0 all-gather.8.cloned.1.call-update
  79.7 0.0 all-gather.10.cloned.1.call-start
  79.7 1.6 copy.28
  81.4 0.6 broadcast_1_keep.2.keep
  81.9 0.0 copy-start.1
  81.9 25.6 %panel.3.rest_0_.rest_1_.first_ref.own_first_ref = f32[4096,256]{1,0:T(8,128)} custom-call(s32[1]{0:T(128)} %bitcast.pivot, s32[16]{0:T(128)} %broadcast_1_keep.2.keep, f32[4096,256]{1,0:T(8,128)} %all-gather.6.cloned.1.call-done.raw_ref.diag_ref, f32[4096,256]{1,0:T(8,128)} %all-gather.6.cloned.1.call-done.raw_ref.diag_ref), custom_call_target="tpu_custom_call" | custom-call | flops 6442450944 | bytes 67108864 | tf_op jit(solution)/shard_map/panel/pallas_call | solution.py:116
  107.5 0.0 copy-done
  107.5 29.7 %all-gather.8.cloned.1.call-done.raw_ref.diag_ref = f32[4096,256]{1,0:T(8,128)} async-done(((f32[256,256]{1,0:T(8,128)}), f32[4096,256]{1,0:T(8,128)}) %all-gather.8.cloned.1.call-update) | async-done | bytes 4194320 | tf_op jit(solution)/shard_map/all_gather | solution.py:251
  137.2 0.0 all-gather.10.cloned.1.call-update
  137.2 0.2 all-gather.12.cloned.1.call-start
  143.3 0.0 copy-done.1
  143.4 1.1 compare_convert_fusion.keep
  144.5 1.7 pad_add_fusion.flags
  146.2 30.0 %panel.4.second_ref.own_second_ref = f32[4096,256]{1,0:T(8,128)} custom-call(s32[1]{0:T(128)} %bitcast.1.pivot, s32[16]{0:T(128)} %compare_convert_fusion.keep, f32[4096,256]{1,0:T(8,128)} %all-gather.8.cloned.1.call-done.raw_ref.diag_ref, f32[4096,256]{1,0:T(8,128)} %all-gather.8.cloned.1.call-done.raw_ref.diag_ref, ...), custom_call_target="tpu_custom_call" | custom-call | flops 6442450944 | bytes 67108864 | tf_op jit(solution)/shard_map/panel/pallas_call | solution.py:116
  176.3 16.3 %update.1 = (f32[4096,256]{1,0:T(8,128)}, f32[16,256,256]{2,1,0:T(8,128)}) custom-call(s32[3]{0:T(128)} %pad_add_fusion.flags, s32[16]{0:T(128)} %bitcast.44, f32[4096,256]{1,0:T(8,128)} %front_ref.1, f32[4096,256]{1,0:T(8,128)} %panel.3.rest_0_.rest_1_.first_ref.own_first_ref, f32[4096,256]{1,0:T(8,128)} %panel.4.second_ref.own_second_ref, ...), custom_call_target="tpu_custom_call" | custom-call | flops 3221225472 | bytes 33554432 | tf_op jit(solution)/shard_map/update/pallas_call | solution.py:186
  192.6 5.4 %all-gather.10.cloned.1.call-done = f32[4096,256]{0,1:T(8,128)} async-done(((f32[256,256]{0,1:T(8,128)}), f32[4096,256]{0,1:T(8,128)}) %all-gather.10.cloned.1.call-update) | async-done | bytes 4194320 | tf_op jit(solution)/shard_map/all_gather | solution.py:258
  198.0 1.4 convolution_subtract_fusion.2
  199.4 1.4 fusion.4
  200.8 0.1 add_bitcast_fusion
  200.9 1.1 add.56
  202.0 0.8 copy.31
  202.8 0.0 all-gather.12.cloned.1.call-update
  202.8 0.0 all-gather.14.cloned.1.call-start
  202.9 34.5 %all-gather.12.cloned.1.call-done = f32[8,256,256]{2,1,0:T(8,128)} async-done(((f32[1,256,256]{2,1,0:T(8,128)}), f32[8,256,256]{2,1,0:T(8,128)}) %all-gather.12.cloned.1.call-update) | async-done | bytes 2097168 | tf_op jit(solution)/shard_map/all_gather | solution.py:278
  237.4 2.5 reduce_sum.19
  239.9 0.0 all-gather.14.cloned.1.call-update
  239.9 0.0 reduce-scatter.4.cloned.1.call-start
  240.0 70.9 %all_to_all.5.tile_ref = f32[16,256,256]{2,1,0:T(8,128)} all-to-all(f32[16,256,256]{2,1,0:T(8,128)} %get-tuple-element.21), channel_id=1, replica_groups=mesh['leaf'=8,'front'=16] {'front'}, dimensions={0} | all-to-all | bytes 8388608 | tf_op jit(solution)/shard_map/all_to_all | solution.py:282
  310.8 11.0 %place.1 = f32[256,4096]{1,0:T(8,128)} custom-call(s32[16]{0:T(128)} %copy-done, f32[16,256,256]{2,1,0:T(8,128)} %all_to_all.5.tile_ref), custom_call_target="tpu_custom_call" | custom-call | tf_op jit(solution)/shard_map/place/pallas_call | solution.py:215
  321.8 3.9 all-gather.14.cloned.1.call-done.raw_ref.diag_ref
  325.7 0.0 reduce-scatter.4.cloned.1.call-update
  325.8 0.1 broadcast_in_dim.42
  325.9 25.6 %panel.5 = f32[4096,256]{1,0:T(8,128)} custom-call(s32[1]{0:T(128)} %bitcast.48, s32[16]{0:T(128)} %broadcast_1_keep.2.keep, f32[4096,256]{1,0:T(8,128)} %all-gather.14.cloned.1.call-done.raw_ref.diag_ref, f32[4096,256]{1,0:T(8,128)} %all-gather.14.cloned.1.call-done.raw_ref.diag_ref), custom_call_target="tpu_custom_call" | custom-call | flops 6442450944 | bytes 67108864 | tf_op jit(solution)/shard_map/panel/pallas_call | solution.py:116
  351.6 25.6 %reduce-scatter.4.cloned.1.call-done = f32[32,4096]{1,0:T(8,128)} async-done(((f32[256,4096]{1,0:T(8,128)}), f32[32,4096]{1,0:T(8,128)}) %reduce-scatter.4.cloned.1.call-update) | async-done | bytes 524304
  377.2 3.0 copy.41
  380.2 5.5 %fusion.3 = f32[4096,1,32]{2,0,1:T(8,128)} fusion(f32[4096,256]{1,0:T(8,128)} %panel.5, f32[32,4096]{0,1:T(8,128)} %copy.41, f32[32,4096]{0,1:T(8,128)S(1)} %bitcast.38, s32[]{:T(128)S(6)} %select_n.73, pred[4096]{0:T(1024)(128)(4,1)S(1)} %broadcast_in_dim.43, pred[]{:T(512)S(6)} %eq.19, s32[]{:T(128)S(6)} %select_n.76), kind=kOutput, calls=%fused_computation.4 | convolution fusion | flops 201850880 | bytes 9474057 | tf_op jit(solution)/shard_map/dot_general | solution.py:290
  385.6 3.0 copy.36
  (2 shorter events, 0.1 us)
Async XLA Ops:
  7.2 72.5 %all-gather.6.cloned.1.call-start = ((), (), s32[]{:S(2)}) async-start(), calls=%async_computation.2 | async-start | bytes 4456448 | tf_op jit(solution)/shard_map/all_gather | solution.py:249
  9.3 98.2 %copy-start = (s32[16]{0:T(128)}, s32[16]{0:T(128)S(1)}, u32[]{:S(2)}) copy-start(s32[16]{0:T(128)S(1)} %select_reduce_fusion.source) | copy-start | bytes 196
  19.9 117.3 %all-gather.8.cloned.1.call-start = ((), (), s32[]{:S(2)}) async-start(), calls=%async_computation.3 | async-start | bytes 4456448 | tf_op jit(solution)/shard_map/all_gather | solution.py:251
  79.7 118.3 %all-gather.10.cloned.1.call-start = ((), (), s32[]{:S(2)}) async-start(), calls=%async_computation.4 | async-start | bytes 4456448 | tf_op jit(solution)/shard_map/all_gather | solution.py:258
  81.9 61.4 %copy-start.1 = (s32[16]{0:T(128)S(1)}, s32[16]{0:T(128)}, u32[]{:S(2)}) copy-start(s32[16]{0:T(128)} %param.9) | copy-start | bytes 196
  137.2 100.2 %all-gather.12.cloned.1.call-start = ((), (), s32[]{:S(2)}) async-start(), calls=%async_computation.5 | async-start | bytes 2359296 | tf_op jit(solution)/shard_map/all_gather | solution.py:278
  202.8 122.9 %all-gather.14.cloned.1.call-start = ((), (), s32[]{:S(2)}) async-start(), calls=%async_computation.6 | async-start | bytes 4456448 | tf_op jit(solution)/shard_map/all_gather | solution.py:280
  239.9 137.3 %reduce-scatter.4.cloned.1.call-start = ((), (), s32[]{:S(2)}) async-start(), calls=%async_computation.7 | async-start | bytes 4718592
Sparse Core Ops, SparseCore 0:
  20.0 59.5 all-gather.5
  82.0 55.0 all-gather.7
  140.0 57.9 all-gather.9
  203.0 34.4 all-gather.11
  240.2 85.4 all-gather.13
  328.0 49.1 reduce-scatter.3

commit v5 on v4

--- a/solution.py
+++ b/solution.py
@@ -225,6 +225,43 @@
     )(inverse, tiles)
 
 
+def finish_kernel(flags, part_ref, root_ref, panel_ref, own_ref, out_ref, turned_ref):
+    width, columns = out_ref.shape
+    size = panel_ref.shape[1]
+    turned_ref[...] = panel_ref[...].T
+    change = product(own_ref[...], turned_ref[...])
+    mine = turned_ref[pl.ds(pl.multiple_of(flags[2] * width, width), width), :]
+    first = flags[0] * size - pl.program_id(0) * columns
+    lanes = lax.broadcasted_iota(jnp.int32, (width, columns), 1)
+    dead = (lanes >= first) & (lanes < first + size)
+    part = jnp.where(dead, 0.0, part_ref[...] + root_ref[...] - change)
+    out_ref[...] = jnp.where(flags[0] == flags[1], mine, part)
+
+
+def finish(part, root_rows, panel, flags):
+    width, rows = part.shape
+    size = panel.shape[1]
+    chunk = 4 * size
+    across = pl.BlockSpec((width, chunk), lambda b, flags: (0, b))
+    return pl.pallas_call(
+        finish_kernel,
+        grid_spec=pltpu.PrefetchScalarGridSpec(
+            num_scalar_prefetch=1,
+            grid=(rows // chunk,),
+            in_specs=[
+                across,
+                across,
+                pl.BlockSpec((chunk, size), lambda b, flags: (b, 0)),
+                pl.BlockSpec((width, size), lambda b, flags: (flags[3], 0)),
+            ],
+            out_specs=across,
+            scratch_shapes=[pltpu.VMEM((size, chunk), jnp.float32)],
+        ),
+        out_shape=jax.ShapeDtypeStruct((width, rows), jnp.float32),
+        name="finish",
+    )(flags, part, root_rows, panel, panel)
+
+
 def block_row(tiles, pivot_block):
     return lax.dynamic_index_in_dim(tiles, pivot_block, 0, keepdims=False)
 
@@ -233,10 +270,9 @@
     order_rows, block_size = leaf_fronts.shape
     block_count = order_rows // block_size
     my_block = lax.axis_index("front").astype(jnp.int32)
-    leaf_index = lax.axis_index("leaf")
+    leaf_index = lax.axis_index("leaf").astype(jnp.int32)
     slice_width = root_front.shape[2]
     block_ids = jnp.arange(block_count, dtype=jnp.int32)
-    own_start = my_block * block_size
 
     tiles = leaf_fronts.reshape(block_count, block_size, block_size)
     first, second = leaf_order[0, 0], leaf_order[0, 1]
@@ -276,23 +312,18 @@
     widened = jnp.zeros_like(share)
     widened = lax.dynamic_update_slice_in_dim(widened, root_share, here, 0)
     shares = lax.all_gather(share + widened, "leaf", axis=0)
+    incoming = lax.all_to_all(outgoing, "front", split_axis=0, concat_axis=0, tiled=True)
+    shares, incoming = lax.optimization_barrier((shares, incoming))
     raw_root = jnp.sum(shares, axis=0)
     raw_root = lax.all_gather(raw_root, "front", axis=0, tiled=True)
-
-    incoming = lax.all_to_all(outgoing, "front", split_axis=0, concat_axis=0, tiled=True)
     gathered = place_tiles(incoming, inverse)
     gathered, raw_root = lax.optimization_barrier((gathered, raw_root))
     part = lax.psum_scatter(gathered, "leaf", scatter_dimension=0, tiled=True)
-    part = part + root_rows
 
     panel = make_panel(raw_root, pivot, everything)
-    own = lax.dynamic_slice_in_dim(panel, own_start + leaf_index * slice_width, slice_width, 0)
-    part = part - jnp.dot(own, panel.T, precision=HIGH)
-    part = part.reshape(slice_width, block_count, block_size)
-    part = jnp.where((block_ids != pivot)[None, :, None], part, 0.0)
-    part = part.reshape(slice_width, order_rows)
-    own_panel = lax.dynamic_slice_in_dim(panel, leaf_index * slice_width, slice_width, 1)
-    root_out = jnp.where(my_block == pivot, own_panel, part.T)
+    own_rows = my_block * (block_size // slice_width) + leaf_index
+    ends = jnp.stack([pivot, my_block, leaf_index, own_rows])
+    root_out = finish(part, root_rows, panel, ends).T
     return (leaf_out, root_out[:, None, :])
 
 

time: 398 us -> 403 us (1.013)
  waiting for transfers between devices: 158 us -> 236 us
  blocking collectives: 70.9 us -> 0 us
  local copies, waits for them, and re-layouts: 15.6 us -> 6.94 us
  Pallas kernels: 109 us -> 115 us
  matrix products: 8.25 us -> 2.84 us
  starting transfers between devices: 0.42 us -> 4.78 us
    all_to_all x1 -> x0, blocking collectives: 70.9 us -> none  [shards(): lax.all_to_all(outgoing, 'front', split_axis=0, concat_axis=0, tiled=True)]
    all_gather x1, waiting for transfers between devices: 3.91 us -> 48.2 us  [shards(): raw_root = lax.all_gather(raw_root, 'front', axis=0, tiled=True)]
    all_gather x1, waiting for transfers between devices: 34.5 us -> 68.4 us  [shards(): shares = lax.all_gather(share + widened, 'leaf', axis=0)]
    reduce_scatter x0 -> x1, waiting for transfers between devices: none -> 27.7 us  [shards(): part = lax.psum_scatter(gathered, 'leaf', scatter_dimension=0, tiled=True)]
    unnamed x7 -> x6, waiting for transfers between devices: 25.7 us -> 0.1 us
    pallas_call x0 -> x1, Pallas kernels: none -> 6.13 us  [finish(): pl.pallas_call(finish_kernel, grid_spec=pltpu.PrefetchScalarGridSpec(num_...]
    dot_general x1 -> x0, matrix products: 5.46 us -> none  [shards(): part = part - jnp.dot(own, panel.T, precision=HIGH)]
    all_to_all x0 -> x1, starting transfers between devices: none -> 4.54 us  [shards(): lax.all_to_all(outgoing, 'front', split_axis=0, concat_axis=0, tiled=True)]
  transfers between devices with their start and end apart: 6 -> 7, of which waited for: 6 -> 6; matrix products, arithmetic and copies ran while one was open for 2% -> 2% of each run, Pallas kernels for 27% -> 27%
where the time goes in v5:
time: 403 us; the launch traced here: 401 us
  waiting for transfers between devices  236 us (59%)
  Pallas kernels  115 us (29%)
  between operations  27.5 us (7%)
  other arithmetic  7.47 us (2%)
  local copies, waits for them, and re-layouts  6.94 us (2%)
  starting transfers between devices  4.78 us (1%)
    pallas_call x3, Pallas kernels, make_panel(): pl.pallas_call(panel_kernel, grid_spec=pltpu.PrefetchScalarGridSpec(num_s...  81.4 us
    all_gather x1, waiting for transfers between devices, shards(): shares = lax.all_gather(share + widened, 'leaf', axis=0)  68.4 us
    all_gather x1, waiting for transfers between devices, shards(): raw_first = lax.all_gather(row_first, 'front', axis=0, tiled=True)  58.9 us
    all_gather x1, waiting for transfers between devices, shards(): raw_root = lax.all_gather(raw_root, 'front', axis=0, tiled=True)  48.2 us
    all_gather x1, waiting for transfers between devices, shards(): raw_second = lax.all_gather(row_second, 'front', axis=0, tiled=True)  30.8 us
    reduce_scatter x1, waiting for transfers between devices, shards(): part = lax.psum_scatter(gathered, 'leaf', scatter_dimension=0, tiled=True)  27.7 us
    pallas_call x1, Pallas kernels, update(): pl.pallas_call(update_kernel, grid_spec=pltpu.PrefetchScalarGridSpec(num_...  16.4 us
    pallas_call x1, Pallas kernels, place_tiles(): pl.pallas_call(place_kernel, grid_spec=pltpu.PrefetchScalarGridSpec(num_s...  11.2 us
  transfers between devices with their start and end apart: 7, of which 6 were waited for; matrix products, arithmetic and copies ran while one was open for 2% of the time, Pallas kernels for 27%

profile of v5, /device:TPU:1, one launch (start us, length us, event | category | flops | bytes accessed | tf_op | source)
XLA Modules:
  0.0 400.9 jit_solution(11591935356737543109)
XLA Ops:
  7.2 0.0 all-gather.6.cloned.1.call-start
  8.5 0.8 select_reduce_fusion.source
  9.3 0.0 copy-start.1
  9.9 0.7 fusion.7
  11.9 1.3 fusion.8
  17.1 1.2 constant_dynamic-slice_fusion
  18.2 0.8 copy.16
  19.1 0.0 all-gather.6.cloned.1.call-update
  19.1 0.0 all-gather.8.cloned.1.call-start
  19.2 0.8 copy.17
  20.0 58.9 %all-gather.6.cloned.1.call-done.raw_ref.diag_ref = f32[4096,256]{1,0:T(8,128)} async-done(((f32[256,256]{1,0:T(8,128)}), f32[4096,256]{1,0:T(8,128)}) %all-gather.6.cloned.1.call-update) | async-done | bytes 4194320 | tf_op jit(solution)/shard_map/all_gather | solution.py:285
  78.9 0.0 all-gather.8.cloned.1.call-update
  78.9 0.0 all-gather.10.cloned.1.call-start
  78.9 0.8 copy.18
  79.8 0.6 broadcast_1_keep.2.keep
  80.4 0.0 copy-start.2
  80.4 25.5 %panel.3.rest_0_.rest_1_.first_ref.own_first_ref = f32[4096,256]{1,0:T(8,128)} custom-call(s32[1]{0:T(128)} %bitcast.pivot, s32[16]{0:T(128)} %broadcast_1_keep.2.keep, f32[4096,256]{1,0:T(8,128)} %all-gather.6.cloned.1.call-done.raw_ref.diag_ref, f32[4096,256]{1,0:T(8,128)} %all-gather.6.cloned.1.call-done.raw_ref.diag_ref), custom_call_target="tpu_custom_call" | custom-call | flops 6442450944 | bytes 67108864 | tf_op jit(solution)/shard_map/panel/pallas_call | solution.py:116
  105.9 0.0 copy-done.1
  105.9 30.8 %all-gather.8.cloned.1.call-done.raw_ref.diag_ref = f32[4096,256]{1,0:T(8,128)} async-done(((f32[256,256]{1,0:T(8,128)}), f32[4096,256]{1,0:T(8,128)}) %all-gather.8.cloned.1.call-update) | async-done | bytes 4194320 | tf_op jit(solution)/shard_map/all_gather | solution.py:287
  136.7 0.0 all-gather.10.cloned.1.call-update
  136.7 0.0 copy-done.2
  142.9 1.1 compare_convert_fusion.keep
  144.0 1.8 pad_add_fusion.flags
  145.8 30.2 %panel.4.second_ref.own_second_ref = f32[4096,256]{1,0:T(8,128)} custom-call(s32[1]{0:T(128)} %bitcast.1.pivot, s32[16]{0:T(128)} %compare_convert_fusion.keep, f32[4096,256]{1,0:T(8,128)} %all-gather.8.cloned.1.call-done.raw_ref.diag_ref, f32[4096,256]{1,0:T(8,128)} %all-gather.8.cloned.1.call-done.raw_ref.diag_ref, ...), custom_call_target="tpu_custom_call" | custom-call | flops 6442450944 | bytes 67108864 | tf_op jit(solution)/shard_map/panel/pallas_call | solution.py:116
  176.0 16.4 %update.1 = (f32[4096,256]{1,0:T(8,128)}, f32[16,256,256]{2,1,0:T(8,128)}) custom-call(s32[3]{0:T(128)} %pad_add_fusion.flags, s32[16]{0:T(128)} %bitcast.46, f32[4096,256]{1,0:T(8,128)} %front_ref.1, f32[4096,256]{1,0:T(8,128)} %panel.3.rest_0_.rest_1_.first_ref.own_first_ref, f32[4096,256]{1,0:T(8,128)} %panel.4.second_ref.own_second_ref, ...), custom_call_target="tpu_custom_call" | custom-call | flops 3221225472 | bytes 33554432 | tf_op jit(solution)/shard_map/update/pallas_call | solution.py:186
  192.3 2.2 all-gather.10.cloned.1.call-done
  194.5 4.5 %all-to-all-start = ((f32[16,256,256]{2,1,0:T(8,128)}), f32[16,256,256]{2,1,0:T(8,128)}, u32[]{:S(2)}, u32[]{:S(2)}) async-start(f32[16,256,256]{2,1,0:T(8,128)} %get-tuple-element.25), calls=%async_computation | async-start | bytes 8388608 | tf_op jit(solution)/shard_map/all_to_all | solution.py:315
  199.1 0.0 all-gather.12.cloned.1.call-start
  199.1 1.5 convolution_subtract_fusion.1
  200.6 1.4 fusion
  202.0 0.8 bitcast_dynamic-update-slice_fusion
  202.8 0.0 copy-start
  202.8 0.7 copy-done
  203.5 0.0 all-gather.12.cloned.1.call-update
  203.5 0.0 all-gather.14.cloned.1.call-start
  203.6 68.4 %all-gather.12.cloned.1.call-done = f32[8,256,256]{2,1,0:T(8,128)} async-done(((f32[1,256,256]{2,1,0:T(8,128)}), f32[8,256,256]{2,1,0:T(8,128)}) %all-gather.12.cloned.1.call-update) | async-done | bytes 2097168 | tf_op jit(solution)/shard_map/all_gather | solution.py:314
  271.9 0.0 all-to-all-done.tile_ref
  271.9 2.5 reduce_sum.19
  274.4 0.0 all-gather.14.cloned.1.call-update
  274.4 0.0 reduce-scatter.2.cloned.1.call-start
  274.5 11.2 %place.1 = f32[256,4096]{1,0:T(8,128)} custom-call(s32[16]{0:T(128)} %copy-done.1, f32[16,256,256]{2,1,0:T(8,128)} %all-to-all-done.tile_ref), custom_call_target="tpu_custom_call" | custom-call | tf_op jit(solution)/shard_map/place/pallas_call | solution.py:215
  285.7 48.2 %all-gather.14.cloned.1.call-done.raw_ref.diag_ref = f32[4096,256]{1,0:T(8,128)} async-done(((f32[256,256]{1,0:T(8,128)}), f32[4096,256]{1,0:T(8,128)}) %all-gather.14.cloned.1.call-update) | async-done | bytes 4194320 | tf_op jit(solution)/shard_map/all_gather | solution.py:318
  333.9 0.0 reduce-scatter.2.cloned.1.call-update
  333.9 0.6 pad_add_fusion.1.flags
  334.5 25.7 %panel.5.panel_ref.own_ref = f32[4096,256]{1,0:T(8,128)} custom-call(s32[1]{0:T(128)} %bitcast.42, s32[16]{0:T(128)} %broadcast_1_keep.2.keep, f32[4096,256]{1,0:T(8,128)} %all-gather.14.cloned.1.call-done.raw_ref.diag_ref, f32[4096,256]{1,0:T(8,128)} %all-gather.14.cloned.1.call-done.raw_ref.diag_ref), custom_call_target="tpu_custom_call" | custom-call | flops 6442450944 | bytes 67108864 | tf_op jit(solution)/shard_map/panel/pallas_call | solution.py:116
  360.2 27.7 %reduce-scatter.2.cloned.1.call-done.part_ref = f32[32,4096]{1,0:T(8,128)} async-done(((f32[256,4096]{1,0:T(8,128)}), f32[32,4096]{1,0:T(8,128)}) %reduce-scatter.2.cloned.1.call-update) | async-done | bytes 524304 | tf_op jit(solution)/shard_map/reduce_scatter | solution.py:321
  387.9 6.1 %finish.1 = f32[32,4096]{1,0:T(8,128)} custom-call(s32[4]{0:T(128)} %pad_add_fusion.1.flags, f32[32,4096]{1,0:T(8,128)} %reduce-scatter.2.cloned.1.call-done.part_ref, f32[32,4096]{1,0:T(8,128)} %bitcast.37, f32[4096,256]{1,0:T(8,128)} %panel.5.panel_ref.own_ref, f32[4096,256]{1,0:T(8,128)} %panel.5.panel_ref.own_ref), custom_call_target="tpu_custom_call" | custom-call | tf_op jit(solution)/shard_map/finish/pallas_call | solution.py:246
  (1 shorter events, 0.0 us)
Async XLA Ops:
  7.2 71.7 %all-gather.6.cloned.1.call-start = ((), (), s32[]{:S(2)}) async-start(), calls=%async_computation.2 | async-start | bytes 4456448 | tf_op jit(solution)/shard_map/all_gather | solution.py:285
  9.3 96.6 %copy-start.1 = (s32[16]{0:T(128)}, s32[16]{0:T(128)S(1)}, u32[]{:S(2)}) copy-start(s32[16]{0:T(128)S(1)} %select_reduce_fusion.source) | copy-start | bytes 196
  19.1 117.6 %all-gather.8.cloned.1.call-start = ((), (), s32[]{:S(2)}) async-start(), calls=%async_computation.3 | async-start | bytes 4456448 | tf_op jit(solution)/shard_map/all_gather | solution.py:287
  78.9 115.6 %all-gather.10.cloned.1.call-start = ((), (), s32[]{:S(2)}) async-start(), calls=%async_computation.4 | async-start | bytes 4456448 | tf_op jit(solution)/shard_map/all_gather | solution.py:294
  80.4 56.4 %copy-start.2 = (s32[16]{0:T(128)S(1)}, s32[16]{0:T(128)}, u32[]{:S(2)}) copy-start(s32[16]{0:T(128)} %param.9) | copy-start | bytes 196
  194.5 77.4 %all-to-all-start = ((f32[16,256,256]{2,1,0:T(8,128)}), f32[16,256,256]{2,1,0:T(8,128)}, u32[]{:S(2)}, u32[]{:S(2)}) async-start(f32[16,256,256]{2,1,0:T(8,128)} %get-tuple-element.25), calls=%async_computation | async-start | bytes 8388608 | tf_op jit(solution)/shard_map/all_to_all | solution.py:315
  199.1 72.9 %all-gather.12.cloned.1.call-start = ((), (), s32[]{:S(2)}) async-start(), calls=%async_computation.5 | async-start | bytes 2359296 | tf_op jit(solution)/shard_map/all_gather | solution.py:314
  202.8 0.7 copy-start
  203.5 130.3 %all-gather.14.cloned.1.call-start = ((), (), s32[]{:S(2)}) async-start(), calls=%async_computation.6 | async-start | bytes 4456448 | tf_op jit(solution)/shard_map/all_gather | solution.py:318
  274.4 113.5 %reduce-scatter.2.cloned.1.call-start = ((), (), s32[]{:S(2)}) async-start(), calls=%async_computation.7 | async-start | bytes 4718592 | tf_op jit(solution)/shard_map/reduce_scatter | solution.py:321
Sparse Core Ops, SparseCore 0:
  19.2 59.5 all-gather.5
  81.8 54.8 all-gather.7
  139.7 54.8 all-gather.9
  203.6 68.2 all-gather.11
  274.8 59.0 all-gather.13
  336.1 51.7 reduce-scatter.1

commit v6 on v5

--- a/solution.py
+++ b/solution.py
@@ -312,10 +312,10 @@
     widened = jnp.zeros_like(share)
     widened = lax.dynamic_update_slice_in_dim(widened, root_share, here, 0)
     shares = lax.all_gather(share + widened, "leaf", axis=0)
-    incoming = lax.all_to_all(outgoing, "front", split_axis=0, concat_axis=0, tiled=True)
-    shares, incoming = lax.optimization_barrier((shares, incoming))
+    shares, outgoing = lax.optimization_barrier((shares, outgoing))
     raw_root = jnp.sum(shares, axis=0)
     raw_root = lax.all_gather(raw_root, "front", axis=0, tiled=True)
+    incoming = lax.all_to_all(outgoing, "front", split_axis=0, concat_axis=0, tiled=True)
     gathered = place_tiles(incoming, inverse)
     gathered, raw_root = lax.optimization_barrier((gathered, raw_root))
     part = lax.psum_scatter(gathered, "leaf", scatter_dimension=0, tiled=True)

time: 403 us -> 390 us (0.968)
  waiting for transfers between devices: 236 us -> 155 us
  blocking collectives: 0 us -> 70.9 us
  starting transfers between devices: 4.78 us -> 0.42 us
    all_to_all x0 -> x1, blocking collectives: none -> 70.9 us  [shards(): lax.all_to_all(outgoing, 'front', split_axis=0, concat_axis=0, tiled=True)]
    all_gather x1, waiting for transfers between devices: 48.2 us -> 3.88 us  [shards(): raw_root = lax.all_gather(raw_root, 'front', axis=0, tiled=True)]
    all_gather x1, waiting for transfers between devices: 68.4 us -> 34.9 us  [shards(): shares = lax.all_gather(share + widened, 'leaf', axis=0)]
    all_to_all x1 -> x0, starting transfers between devices: 4.54 us -> none  [shards(): lax.all_to_all(outgoing, 'front', split_axis=0, concat_axis=0, tiled=True)]
  transfers between devices with their start and end apart: 7 -> 6, of which waited for: 6 -> 6; matrix products, arithmetic and copies ran while one was open for 2% -> 2% of each run, Pallas kernels for 27% -> 28%
where the time goes in v6:
time: 390 us; the launch traced here: 388 us
  waiting for transfers between devices  155 us (40%)
  Pallas kernels  115 us (29%)
  blocking collectives  70.9 us (18%)
  between operations  28.6 us (7%)
  other arithmetic  7.69 us (2%)
  local copies, waits for them, and re-layouts  7.04 us (2%)
    pallas_call x3, Pallas kernels, make_panel(): pl.pallas_call(panel_kernel, grid_spec=pltpu.PrefetchScalarGridSpec(num_s...  81.3 us
    all_to_all x1, blocking collectives, shards(): lax.all_to_all(outgoing, 'front', split_axis=0, concat_axis=0, tiled=True)  70.9 us
    all_gather x1, waiting for transfers between devices, shards(): raw_first = lax.all_gather(row_first, 'front', axis=0, tiled=True)  58.9 us
    all_gather x1, waiting for transfers between devices, shards(): shares = lax.all_gather(share + widened, 'leaf', axis=0)  34.9 us
    all_gather x1, waiting for transfers between devices, shards(): raw_second = lax.all_gather(row_second, 'front', axis=0, tiled=True)  31 us
    reduce_scatter x1, waiting for transfers between devices, shards(): part = lax.psum_scatter(gathered, 'leaf', scatter_dimension=0, tiled=True)  25.2 us
    pallas_call x1, Pallas kernels, update(): pl.pallas_call(update_kernel, grid_spec=pltpu.PrefetchScalarGridSpec(num_...  16.5 us
    pallas_call x1, Pallas kernels, place_tiles(): pl.pallas_call(place_kernel, grid_spec=pltpu.PrefetchScalarGridSpec(num_s...  11 us
  transfers between devices with their start and end apart: 6, of which 6 were waited for; matrix products, arithmetic and copies ran while one was open for 2% of the time, Pallas kernels for 28%

profile of v6, /device:TPU:1, one launch (start us, length us, event | category | flops | bytes accessed | tf_op | source)
XLA Modules:
  0.0 387.7 jit_solution(1037194348553469363)
XLA Ops:
  7.2 0.0 all-gather.6.cloned.1.call-start
  8.5 0.8 select_reduce_fusion.source
  9.3 0.0 copy-start.1
  9.9 0.7 fusion.7
  11.9 1.4 fusion.8
  17.8 1.2 constant_dynamic-slice_fusion
  19.0 0.8 copy.16
  19.8 0.0 all-gather.6.cloned.1.call-update
  19.9 0.0 all-gather.8.cloned.1.call-start
  19.9 0.8 copy.17
  20.8 58.9 %all-gather.6.cloned.1.call-done.raw_ref.diag_ref = f32[4096,256]{1,0:T(8,128)} async-done(((f32[256,256]{1,0:T(8,128)}), f32[4096,256]{1,0:T(8,128)}) %all-gather.6.cloned.1.call-update) | async-done | bytes 4194320 | tf_op jit(solution)/shard_map/all_gather | solution.py:285
  79.6 0.0 all-gather.8.cloned.1.call-update
  79.6 0.0 all-gather.10.cloned.1.call-start
  79.7 0.8 copy.18
  80.5 0.6 broadcast_1_keep.2.keep
  81.1 0.0 copy-start.2
  81.1 25.6 %panel.3.rest_0_.rest_1_.first_ref.own_first_ref = f32[4096,256]{1,0:T(8,128)} custom-call(s32[1]{0:T(128)} %bitcast.pivot, s32[16]{0:T(128)} %broadcast_1_keep.2.keep, f32[4096,256]{1,0:T(8,128)} %all-gather.6.cloned.1.call-done.raw_ref.diag_ref, f32[4096,256]{1,0:T(8,128)} %all-gather.6.cloned.1.call-done.raw_ref.diag_ref), custom_call_target="tpu_custom_call" | custom-call | flops 6442450944 | bytes 67108864 | tf_op jit(solution)/shard_map/panel/pallas_call | solution.py:116
  106.7 0.0 copy-done.1
  106.7 31.0 %all-gather.8.cloned.1.call-done.raw_ref.diag_ref = f32[4096,256]{1,0:T(8,128)} async-done(((f32[256,256]{1,0:T(8,128)}), f32[4096,256]{1,0:T(8,128)}) %all-gather.8.cloned.1.call-update) | async-done | bytes 4194320 | tf_op jit(solution)/shard_map/all_gather | solution.py:287
  137.7 0.0 all-gather.10.cloned.1.call-update
  137.7 0.2 all-gather.12.cloned.1.call-start
  138.0 0.0 copy-done.2
  144.6 1.1 compare_convert_fusion.keep
  145.7 2.0 pad_add_fusion.flags
  147.7 30.1 %panel.4.second_ref.own_second_ref = f32[4096,256]{1,0:T(8,128)} custom-call(s32[1]{0:T(128)} %bitcast.1.pivot, s32[16]{0:T(128)} %compare_convert_fusion.keep, f32[4096,256]{1,0:T(8,128)} %all-gather.8.cloned.1.call-done.raw_ref.diag_ref, f32[4096,256]{1,0:T(8,128)} %all-gather.8.cloned.1.call-done.raw_ref.diag_ref, ...), custom_call_target="tpu_custom_call" | custom-call | flops 6442450944 | bytes 67108864 | tf_op jit(solution)/shard_map/panel/pallas_call | solution.py:116
  177.8 16.5 %update.1 = (f32[4096,256]{1,0:T(8,128)}, f32[16,256,256]{2,1,0:T(8,128)}) custom-call(s32[3]{0:T(128)} %pad_add_fusion.flags, s32[16]{0:T(128)} %bitcast.46, f32[4096,256]{1,0:T(8,128)} %front_ref.1, f32[4096,256]{1,0:T(8,128)} %panel.3.rest_0_.rest_1_.first_ref.own_first_ref, f32[4096,256]{1,0:T(8,128)} %panel.4.second_ref.own_second_ref, ...), custom_call_target="tpu_custom_call" | custom-call | flops 3221225472 | bytes 33554432 | tf_op jit(solution)/shard_map/update/pallas_call | solution.py:186
  194.2 1.4 all-gather.10.cloned.1.call-done
  195.6 1.5 convolution_subtract_fusion.1
  197.1 1.4 fusion
  198.5 0.8 bitcast_dynamic-update-slice_fusion
  199.2 0.0 copy-start
  199.2 0.7 copy-done
  199.9 0.0 all-gather.12.cloned.1.call-update
  200.0 0.0 all-gather.14.cloned.1.call-start
  200.0 34.9 %all-gather.12.cloned.1.call-done = f32[8,256,256]{2,1,0:T(8,128)} async-done(((f32[1,256,256]{2,1,0:T(8,128)}), f32[8,256,256]{2,1,0:T(8,128)}) %all-gather.12.cloned.1.call-update) | async-done | bytes 2097168 | tf_op jit(solution)/shard_map/all_gather | solution.py:314
  235.0 2.5 reduce_sum.19
  237.4 0.0 all-gather.14.cloned.1.call-update
  237.4 0.0 reduce-scatter.2.cloned.1.call-start
  237.5 70.9 %all_to_all.5.tile_ref = f32[16,256,256]{2,1,0:T(8,128)} all-to-all(f32[16,256,256]{2,1,0:T(8,128)} %get-tuple-element.26), channel_id=1, replica_groups=mesh['leaf'=8,'front'=16] {'front'}, dimensions={0} | all-to-all | bytes 8388608 | tf_op jit(solution)/shard_map/all_to_all | solution.py:318
  308.4 11.0 %place.1 = f32[256,4096]{1,0:T(8,128)} custom-call(s32[16]{0:T(128)} %copy-done.1, f32[16,256,256]{2,1,0:T(8,128)} %all_to_all.5.tile_ref), custom_call_target="tpu_custom_call" | custom-call | tf_op jit(solution)/shard_map/place/pallas_call | solution.py:215
  319.4 3.9 %all-gather.14.cloned.1.call-done.raw_ref.diag_ref = f32[4096,256]{1,0:T(8,128)} async-done(((f32[256,256]{1,0:T(8,128)}), f32[4096,256]{1,0:T(8,128)}) %all-gather.14.cloned.1.call-update) | async-done | bytes 4194320 | tf_op jit(solution)/shard_map/all_gather | solution.py:317
  323.3 0.0 reduce-scatter.2.cloned.1.call-update
  323.3 0.6 pad_add_fusion.1.flags
  323.9 25.6 %panel.5.panel_ref.own_ref = f32[4096,256]{1,0:T(8,128)} custom-call(s32[1]{0:T(128)} %bitcast.42, s32[16]{0:T(128)} %broadcast_1_keep.2.keep, f32[4096,256]{1,0:T(8,128)} %all-gather.14.cloned.1.call-done.raw_ref.diag_ref, f32[4096,256]{1,0:T(8,128)} %all-gather.14.cloned.1.call-done.raw_ref.diag_ref), custom_call_target="tpu_custom_call" | custom-call | flops 6442450944 | bytes 67108864 | tf_op jit(solution)/shard_map/panel/pallas_call | solution.py:116
  349.5 25.2 %reduce-scatter.2.cloned.1.call-done.part_ref = f32[32,4096]{1,0:T(8,128)} async-done(((f32[256,4096]{1,0:T(8,128)}), f32[32,4096]{1,0:T(8,128)}) %reduce-scatter.2.cloned.1.call-update) | async-done | bytes 524304 | tf_op jit(solution)/shard_map/reduce_scatter | solution.py:321
  374.7 6.1 %finish.1 = f32[32,4096]{1,0:T(8,128)} custom-call(s32[4]{0:T(128)} %pad_add_fusion.1.flags, f32[32,4096]{1,0:T(8,128)} %reduce-scatter.2.cloned.1.call-done.part_ref, f32[32,4096]{1,0:T(8,128)} %bitcast.37, f32[4096,256]{1,0:T(8,128)} %panel.5.panel_ref.own_ref, f32[4096,256]{1,0:T(8,128)} %panel.5.panel_ref.own_ref), custom_call_target="tpu_custom_call" | custom-call | tf_op jit(solution)/shard_map/finish/pallas_call | solution.py:246
  (1 shorter events, 0.0 us)
Async XLA Ops:
  7.2 72.5 %all-gather.6.cloned.1.call-start = ((), (), s32[]{:S(2)}) async-start(), calls=%async_computation.2 | async-start | bytes 4456448 | tf_op jit(solution)/shard_map/all_gather | solution.py:285
  9.3 97.4 %copy-start.1 = (s32[16]{0:T(128)}, s32[16]{0:T(128)S(1)}, u32[]{:S(2)}) copy-start(s32[16]{0:T(128)S(1)} %select_reduce_fusion.source) | copy-start | bytes 196
  19.9 117.8 %all-gather.8.cloned.1.call-start = ((), (), s32[]{:S(2)}) async-start(), calls=%async_computation.3 | async-start | bytes 4456448 | tf_op jit(solution)/shard_map/all_gather | solution.py:287
  79.6 115.9 %all-gather.10.cloned.1.call-start = ((), (), s32[]{:S(2)}) async-start(), calls=%async_computation.4 | async-start | bytes 4456448 | tf_op jit(solution)/shard_map/all_gather | solution.py:294
  81.1 56.9 %copy-start.2 = (s32[16]{0:T(128)S(1)}, s32[16]{0:T(128)}, u32[]{:S(2)}) copy-start(s32[16]{0:T(128)} %param.9) | copy-start | bytes 196
  137.7 97.2 %all-gather.12.cloned.1.call-start = ((), (), s32[]{:S(2)}) async-start(), calls=%async_computation.5 | async-start | bytes 2359296 | tf_op jit(solution)/shard_map/all_gather | solution.py:314
  199.2 0.7 copy-start
  200.0 123.3 %all-gather.14.cloned.1.call-start = ((), (), s32[]{:S(2)}) async-start(), calls=%async_computation.6 | async-start | bytes 4456448 | tf_op jit(solution)/shard_map/all_gather | solution.py:317
  237.4 137.3 %reduce-scatter.2.cloned.1.call-start = ((), (), s32[]{:S(2)}) async-start(), calls=%async_computation.7 | async-start | bytes 4718592 | tf_op jit(solution)/shard_map/reduce_scatter | solution.py:321
Sparse Core Ops, SparseCore 0:
  20.0 59.5 all-gather.5
  82.6 55.0 all-gather.7
  140.7 54.8 all-gather.9
  200.1 34.8 all-gather.11
  237.8 85.4 all-gather.13
  325.5 49.1 reduce-scatter.1
